TPU v7x, 32 devices: a whole 2x2x4 slice. The times are simulated.
32 devices in a mesh: dp: 8 (over y, x, core), vocab: 4 (over z).
Axes of the slice: x: 2, y: 2, z: 4, core: 2. Of those that a mesh axis runs over, the one named last changes fastest.
Arguments:
- hidden: bfloat16 [128, 5120], P('dp', 'vocab')
- inputs: bfloat16 [128, 3072], P('dp', 'vocab'), may hold values from -6 to 6
- gain: float32 [5120], replicated, may hold values from 0.5 to 1.5
- unembed: bfloat16 [6400, 5120], P(('dp', 'vocab'))
- proj_out: bfloat16 [5120, 128], replicated, may hold values from -6 to 6
- proj_in: bfloat16 [3072, 128], replicated, may hold values from -0.109375 to 0.109375
- targets: int32 [128], replicated, may hold values from 0 to 6399
- segment_ids: int32 [128], replicated, may hold values from 0 to 3, never falling along the last dimension, each value on 1 to 96 neighbouring positions
- store: bfloat16 [2048, 16384], P(('dp', 'vocab')), may hold values from -0.005859375 to 0.005859375
Outputs:
- scores: float32 [4, 2048], P(None, ('dp', 'vocab'))
- logprob: float32 [128], P('dp')
Inputs may be any that keep to these rules, and one draw needn't show every extreme that they name: `segment_ids`: each sequence is a run of consecutive tokens; ids never fall; each sequence has 1 to 96 tokens and one has exactly 96.
All inputs are finite; a program needn't handle non-finite values.
Results may differ from a plain program's by a relative error of at most 0.0074.
Values may be sent and summed in bfloat16 or wider, within the bound.
No kernel may reach another device: no remote copies, remote signals or barrier semaphores. Data moves between devices by JAX's collectives and lax.ppermute only.
A program may use at most 64 MiB of HBM per device.

v0:
```python
import functools

import jax
import jax.numpy as jnp
from jax import lax
from jax.experimental import pallas as pl
from jax.experimental.pallas import tpu as pltpu
from jax.sharding import PartitionSpec as P


EPSILON = 1e-06
AXES = ("dp", "vocab")
F32 = jnp.float32
BF16 = jnp.bfloat16


VMEM = pl.BlockSpec(memory_space=pltpu.VMEM)
HBM = pl.BlockSpec(memory_space=pltpu.HBM)


def split(x):
    high = x.astype(BF16)
    return high, (x - high.astype(F32)).astype(BF16)


def dot(a, b, dims=((1,), (0,))):
    return lax.dot_general(a, b, (dims, ((), ())), preferred_element_type=F32)


def call(kernel, out_shape, n_in, hbm_at=(), scratch=(), us=1.0):
    specs = [HBM if i in hbm_at else VMEM for i in range(n_in)]
    outs = jax.tree.map(lambda _: VMEM, out_shape)
    run = pl.pallas_call(
        kernel,
        out_shape=out_shape,
        in_specs=specs,
        out_specs=outs,
        scratch_shapes=list(scratch),
        cost_estimate=pl.CostEstimate(flops=0, transcendentals=0, bytes_accessed=int(us * 3_000_000)),
        compiler_params=pltpu.CompilerParams(vmem_limit_bytes=32 * 1024 * 1024),
    )

    def placed(*args):
        return run(
            *[pltpu.with_memory_space_constraint(x, pltpu.HBM) if i in hbm_at else x for i, x in enumerate(args)]
        )

    return placed


def stage_kernel(hidden_hbm, gain_hbm, hidden, gain, sems):
    copies = [
        pltpu.make_async_copy(hidden_hbm, hidden, sems.at[0]),
        pltpu.make_async_copy(gain_hbm, gain, sems.at[1]),
    ]
    for copy in copies:
        copy.start()
    for copy in copies:
        copy.wait()


def norm_kernel(offsets, *refs):
    pieces, gain, normed, root_mean = refs[:-3], refs[-3], refs[-2], refs[-1]
    squares, features = 0.0, 0
    for piece in pieces:
        wide = piece[...].astype(F32)
        squares = squares + jnp.sum(wide * wide, axis=1, keepdims=True)
        features += wide.shape[1]
    root = jnp.sqrt(squares / features + EPSILON)
    inverse = 1.0 / root
    for piece, offset in zip(pieces, offsets, strict=True):
        width = piece.shape[1]
        here = pl.ds(pl.multiple_of(offset(), 128), width)
        normed[:, here] = (piece[...].astype(F32) * gain[:, here] * inverse).astype(BF16)
    wide_root = jnp.broadcast_to(root, (root.shape[0], 128))
    chunks, rows, _ = root_mean.shape
    for c in range(chunks):
        root_mean[c] = wide_root[c * rows : (c + 1) * rows]


def side_kernel(offsets, *refs):
    n = len(offsets)
    pieces = refs[:n]
    sources, gain = refs[n : n + 5], refs[n + 5]
    weights, in_part, hidden_proj, target_column = refs[n + 6 : n + 10]
    buffers, sems = refs[n + 10 : n + 15], refs[n + 15]
    copies = [
        pltpu.make_async_copy(source, buffer, sems.at[i])
        for i, (source, buffer) in enumerate(zip(sources, buffers, strict=True))
    ]
    for copy in copies:
        copy.start()
    proj_out, unembed, proj_in, inputs, targets = buffers
    copies[0].wait()
    total = 0.0
    for piece, offset in zip(pieces, offsets, strict=True):
        width = piece.shape[1]
        total = total + dot(piece[...], proj_out[pl.ds(pl.multiple_of(offset(), 16), width), :])
    copies[1].wait()
    scaled_high, scaled_low = split(unembed[...].astype(F32) * gain[...])
    weights[...] = dot(scaled_high, proj_out[...]) + dot(scaled_low, proj_out[...])
    for copy in copies[2:]:
        copy.wait()
    tokens = targets.shape[1]
    target_column[...] = jnp.broadcast_to(targets[...].astype(F32), (128, tokens)).T
    width = inputs.shape[1]
    start = pl.multiple_of(lax.axis_index("vocab") * width, 16)
    part = dot(inputs[...], proj_in[pl.ds(start, width), :])
    chunks, rows, _ = in_part.shape
    for c in range(chunks):
        in_part[c] = part[c * rows : (c + 1) * rows]
        hidden_proj[c] = total[c * rows : (c + 1) * rows]


def logits_kernel(order, *refs):
    n = len(order)
    pieces = refs[:n]
    unembed, target_column, weights, in_part, out, placed = refs[n:]
    rows = pieces[0].shape[0]
    relative = dot(jnp.concatenate([piece[...] for piece in pieces], axis=0), unembed[...], ((1,), (1,)))
    for k, token_at in enumerate(order):
        placed[pl.ds(pl.multiple_of(token_at(), 16), rows), :] = relative[k * rows : (k + 1) * rows]
    logits = placed[...]
    tokens = logits.shape[0]
    entries = logits.shape[1]
    place = lax.axis_index("dp") * lax.axis_size("vocab") + lax.axis_index("vocab")
    column = lax.broadcasted_iota(jnp.int32, logits.shape, 1) + place * entries
    onehot = target_column[:, 0:1] == column.astype(F32)
    peak = jnp.max(logits, axis=1, keepdims=True)
    shifted = logits - peak
    other = jnp.where(onehot, 0.0, jnp.exp(shifted))
    total = jnp.sum(other, axis=1, keepdims=True)
    moment = jnp.sum(other * shifted, axis=1, keepdims=True)
    target_logit = jnp.sum(jnp.where(onehot, logits, 0.0), axis=1, keepdims=True)
    w_high, w_low = split(weights[...])
    p_high, p_low = split(other)
    sums = dot(p_high, w_high) + (dot(p_high, w_low) + dot(p_low, w_high))
    hot = onehot.astype(F32).astype(BF16)
    target_row = dot(hot, w_high) + dot(hot, w_low)
    lane = lax.broadcasted_iota(jnp.int32, (tokens, 128), 1)
    which = (lane // 2) % 4
    stats = jnp.where(which < 2, jnp.where(which == 0, peak, total), jnp.where(which == 2, moment, target_logit))
    high = stats.astype(BF16).astype(F32)
    middle = (stats - high).astype(BF16).astype(F32)
    low = stats - high - middle
    piece = (lane // 8) % 4
    stats = jnp.where(piece == 0, high, jnp.where(piece == 1, middle, jnp.where(piece == 2, low, 0.0)))
    chunks, rows = out.shape[0], tokens // out.shape[0]
    own = in_part.shape[0]
    mine = lax.axis_index("dp")
    block = lax.broadcasted_iota(jnp.int32, (rows, 128), 1) // (128 // own)
    for d in range(chunks // own):
        row_stats = stats[d * own * rows : (d * own + 1) * rows]
        for k in range(1, own):
            c = d * own + k
            row_stats = jnp.where(block == k, stats[c * rows : (c + 1) * rows], row_stats)
        for k in range(own):
            c = d * own + k
            here = slice(c * rows, (c + 1) * rows)
            terms = jnp.where(mine == d, in_part[k], 0.0)
            out[c] = jnp.concatenate([sums[here], target_row[here], terms, row_stats], axis=0).astype(BF16)


def merge_kernel(features, parts, hidden_projs, root_means, out, logprob):
    index, own = lax.axis_index("vocab"), lax.axis_size("vocab")
    hidden_proj = hidden_projs[index]
    root_mean = root_means[index]
    chunks, rows = parts.shape[0], hidden_proj.shape[0]
    received = parts[...].astype(F32)
    stats = received[:, 3 * rows : 4 * rows].reshape(chunks * rows, 128)
    stats = stats + pltpu.roll(stats, 128 - 8, 1) + pltpu.roll(stats, 128 - 16, 1)
    shape = (chunks, rows, 128)
    peak, total = stats.reshape(shape), pltpu.roll(stats, 128 - 2, 1).reshape(shape)
    moment = pltpu.roll(stats, 128 - 4, 1).reshape(shape)
    target_logit = jnp.sum(pltpu.roll(stats, 128 - 6, 1).reshape(shape), axis=0)
    row_peak = jnp.max(peak, axis=0)
    scale = jnp.exp(peak - row_peak[None])
    row_total = jnp.sum(scale * total, axis=0) + jnp.exp(target_logit - row_peak)
    weight = scale / row_total[None]
    rest = jnp.sum(weight * total, axis=0)
    slope = jnp.sum(weight * (total * (target_logit[None] - peak) - moment), axis=0)
    log_of = target_logit - row_peak - jnp.log(row_total)
    group = 128 // own
    lane = lax.broadcasted_iota(jnp.int32, (rows, 128), 1)
    row = lax.broadcasted_iota(jnp.int32, (rows, 128), 0)
    spread = jnp.zeros((rows, 128), F32)
    for k in range(own):
        spread = jnp.where(lane == k * rows + row, log_of[:, k * group : k * group + 1], spread)
    logprob[...] = jnp.sum(spread, axis=0, keepdims=True)[:, 0 : logprob.shape[1]]

    def pick(x):
        at = lax.broadcasted_iota(jnp.int32, x.shape, x.ndim - 1) == index * group
        return jnp.sum(jnp.where(at, x, 0.0), axis=-1, keepdims=True)

    weight, rest, slope = pick(weight), pick(rest), pick(slope)
    target_row = jnp.sum(received[:, rows : 2 * rows], axis=0)
    grad_proj = rest * target_row - jnp.sum(weight * received[:, 0:rows], axis=0)
    grad_dot = root_mean * slope
    out_grad = grad_proj / root_mean - hidden_proj * (
        grad_dot / (features * (root_mean * root_mean * root_mean))
    )
    in_proj = jnp.sum(received[:, 2 * rows : 3 * rows], axis=0)
    both = jnp.concatenate([out_grad, in_proj], axis=0).astype(BF16)
    out[...] = jnp.broadcast_to(both[None], out.shape)


def scores_kernel(parts, segments, store, scores, out_grad, in_proj, spread, flat):
    chunks, rows = parts.shape[0], parts.shape[1] // 2
    for c in range(chunks):
        both = parts[c].astype(F32)
        here = slice(c * rows, (c + 1) * rows)
        out_grad[here, :] = both[0:rows]
        in_proj[here, :] = both[rows : 2 * rows]
    turned = out_grad[...].T
    tokens = turned.shape[1]
    seqs = flat.shape[0]
    member = (segments[...] == lax.broadcasted_iota(jnp.int32, (seqs, tokens), 0)).astype(F32)
    for p in range(turned.shape[0]):
        spread[p * seqs : (p + 1) * seqs, :] = turned[p : p + 1, :] * member
    grads = dot(spread[...].astype(BF16), in_proj[...].astype(BF16))
    width = grads.shape[1]
    for p in range(turned.shape[0]):
        flat[:, p * width : (p + 1) * width] = grads[p * seqs : (p + 1) * seqs, :]
    result = dot(flat[...].astype(BF16), store[...], ((1,), (1,)))
    scores[...] = result[0 : scores.shape[0], :]


def swap(x, size, mask):
    vocab = size["vocab"]
    count = size["dp"] * vocab
    return lax.ppermute(x, AXES, [(i, i ^ mask) for i in range(count)])


def body(size, *args):
    return steps(size, *args)


def steps(size, hidden, inputs, gain, unembed, proj_out, proj_in, targets, segment_ids, store):
    n_dp, n_vocab = size["dp"], size["vocab"]
    devices = n_dp * n_vocab
    tokens, features = targets.shape[0], gain.shape[0]
    per_device = tokens // devices
    rows, width = hidden.shape
    seqs = tokens // 32
    entries = unembed.shape[0]
    projected = proj_out.shape[1]
    gain_row = gain.reshape(1, features)

    sds = jax.ShapeDtypeStruct
    row_shape = sds((n_vocab, per_device, projected), F32)

    def norm(row_pieces, offsets, gain_row):
        return call(
            functools.partial(norm_kernel, offsets), (sds((rows, features), BF16), row_shape), len(row_pieces) + 1
        )(*row_pieces, gain_row)

    def side_work(row_pieces, offsets, gain_row):
        n = len(row_pieces)
        sources = (proj_out, unembed, proj_in, inputs, targets.reshape(1, tokens))
        return call(
            functools.partial(side_kernel, offsets),
            (sds((entries, projected), F32), row_shape, row_shape, sds((tokens, 128), F32)),
            n + 6,
            hbm_at=range(n, n + 5),
            scratch=[pltpu.VMEM(x.shape, x.dtype) for x in sources] + [pltpu.SemaphoreType.DMA((5,))],
            us=4.0,
        )(*row_pieces, *sources, gain_row)

    if n_dp == 8 and n_vocab == 4 and width % 128 == 0:
        row_pieces = [swap(hidden, size, k) for k in (2, 3, 1)]
        staged, gain_row = call(
            stage_kernel,
            (sds(hidden.shape, BF16), sds(gain_row.shape, F32)),
            2,
            hbm_at=(0, 1),
            scratch=[pltpu.SemaphoreType.DMA((2,))],
        )(hidden, gain_row)
        row_pieces = [staged] + row_pieces
        offsets = [lambda k=k: (lax.axis_index("vocab") ^ k) * width for k in (0, 2, 3, 1)]
        normed, root_mean = norm(row_pieces, offsets, gain_row)
        near = {0: normed}
        for r in (6, 2, 4):
            near[r] = swap(normed, size, r * n_vocab)
        *row_pieces, _ = lax.optimization_barrier((*row_pieces, normed))
        side = side_work(row_pieces, offsets, gain_row)
        near[2], near[4], near[6], side = lax.optimization_barrier((near[2], near[4], near[6], side))
        pieces = dict(near)
        for r in (0, 6, 2, 4):
            pieces[r + 1] = swap(near[r], size, n_vocab)
        pieces = [pieces[r] for r in range(n_dp)]
        order = [lambda r=r: (lax.axis_index("dp") ^ r) * rows for r in range(n_dp)]
    else:
        row_pieces = [lax.all_gather(hidden, "vocab", axis=1, tiled=True)]
        offsets = [lambda: 0]
        normed, root_mean = norm(row_pieces, offsets, gain_row)
        side = side_work(row_pieces, offsets, gain_row)
        pieces = [lax.all_gather(normed, "dp", axis=0, tiled=True)]
        order = [lambda: 0]
    weights, in_part, hidden_proj, target_column = side
    partial = call(
        functools.partial(logits_kernel, order),
        sds((devices, 4 * per_device, projected), BF16),
        len(pieces) + 4,
        scratch=[pltpu.VMEM((tokens, entries), F32)],
        us=2.0,
    )(*pieces, unembed, target_column, weights, in_part)
    partial = lax.all_to_all(partial, AXES, 0, 0, tiled=True)
    merged, logprob = call(
        functools.partial(merge_kernel, features),
        (sds((devices, 2 * per_device, projected), BF16), sds((1, rows), F32)),
        3,
    )(partial, hidden_proj, root_mean)
    merged = lax.all_to_all(merged, AXES, 0, 0, tiled=True)
    padded = -(-seqs // 8) * 8
    scores = call(
        scores_kernel,
        sds((seqs, store.shape[0]), F32),
        3,
        scratch=(
            pltpu.VMEM((tokens, projected), F32),
            pltpu.VMEM((tokens, projected), F32),
            pltpu.VMEM((projected * padded, tokens), F32),
            pltpu.VMEM((padded, store.shape[1]), F32),
        ),
    )(merged, segment_ids.reshape(1, tokens), store)
    return scores, logprob.reshape(rows)


def solution(mesh):
    size = dict(mesh.shape)
    in_specs = (
        P("dp", "vocab"),
        P("dp", "vocab"),
        P(),
        P(AXES, None),
        P(),
        P(),
        P(),
        P(),
        P(AXES, None),
    )
    out_specs = (P(None, AXES), P("dp"))
    return jax.shard_map(
        functools.partial(body, size), mesh=mesh, in_specs=in_specs, out_specs=out_specs, check_vma=False
    )
```

profile of v0, /device:TPU:0, one launch (start us, length us, event | category | flops | bytes accessed | tf_op | source)
XLA Modules:
  0.0 46.9 jit_solution(5972416693062037150)
XLA Ops:
  0.6 4.1 %collective-permute-start = (bf16[16,1280]{1,0:T(8,128)(2,1)}, bf16[16,1280]{1,0:T(8,128)(2,1)S(1)}, u32[]{:S(2)}, u32[]{:S(2)}) collective-permute-start(bf16[16,1280]{1,0:T(8,128)(2,1)} %hidden_hbm.1), channel_id=1, source_target_pairs={{0,2},{1,3},{2,0},{3,1},{4,6},{5,7},{6,4},{7,5},{8,10},{9,11},{10,... | collective-permute-start | bytes 122888 | tf_op jit(solution)/shard_map/ppermute | solution.py:231
  4.8 1.6 %collective-permute-start.2 = (bf16[16,1280]{1,0:T(8,128)(2,1)}, bf16[16,1280]{1,0:T(8,128)(2,1)S(1)}, u32[]{:S(2)}, u32[]{:S(2)}) collective-permute-start(bf16[16,1280]{1,0:T(8,128)(2,1)} %hidden_hbm.1), channel_id=1, source_target_pairs={{0,1},{1,0},{2,3},{3,2},{4,5},{5,4},{6,7},{7,6},{8,9},{9,8},{10,11... | collective-permute-start | bytes 122888 | tf_op jit(solution)/shard_map/ppermute | solution.py:231
  6.3 0.0 collective-permute-start.1
  6.3 0.9 %shard_map.104 = (bf16[16,1280]{1,0:T(8,128)(2,1)S(1)}, f32[1,5120]{1,0:T(1,128)S(1)}) custom-call(bf16[16,1280]{1,0:T(8,128)(2,1)} %hidden_hbm.1, f32[1,5120]{1,0:T(1,128)} %bitcast.5), custom_call_target="tpu_custom_call" | custom-call | bytes 3000000 | tf_op jit(solution)/shard_map/pallas_call | solution.py:44
  7.2 0.3 collective-permute-done.refs_1_
  7.5 1.5 %collective-permute-done.2.refs_3_ = bf16[16,1280]{1,0:T(8,128)(2,1)S(1)} collective-permute-done((bf16[16,1280]{1,0:T(8,128)(2,1)}, bf16[16,1280]{1,0:T(8,128)(2,1)S(1)}, u32[]{:S(2)}, u32[]{:S(2)}) %collective-permute-start.2) | collective-permute-done | bytes 40992 | tf_op jit(solution)/shard_map/ppermute | solution.py:231
  9.0 3.4 %collective-permute-done.1.refs_2_ = bf16[16,1280]{1,0:T(8,128)(2,1)S(1)} collective-permute-done((bf16[16,1280]{1,0:T(8,128)(2,1)}, bf16[16,1280]{1,0:T(8,128)(2,1)S(1)}, u32[]{:S(2)}, u32[]{:S(2)}) %collective-permute-start.1) | collective-permute-done | bytes 40992 | tf_op jit(solution)/shard_map/ppermute | solution.py:231
  12.3 0.2 shard_map.105
  12.5 2.5 %collective-permute-start.6 = (bf16[16,5120]{1,0:T(8,128)(2,1)S(1)}, bf16[16,5120]{1,0:T(8,128)(2,1)S(1)}, u32[]{:S(2)}, u32[]{:S(2)}) collective-permute-start(bf16[16,5120]{1,0:T(8,128)(2,1)S(1)} %get-tuple-element.25.refs_0_), channel_id=1, source_target_pairs={{0,24},{1,25},{2,26},{3,27},{4,28},{5,29},{6,30},{7,31},{8,16},{9,... | collective-permute-start | bytes 491528 | tf_op jit(solution)/shard_map/ppermute | solution.py:231
  15.0 0.5 %collective-permute-start.5 = (bf16[16,5120]{1,0:T(8,128)(2,1)S(1)}, bf16[16,5120]{1,0:T(8,128)(2,1)S(1)}, u32[]{:S(2)}, u32[]{:S(2)}) collective-permute-start(bf16[16,5120]{1,0:T(8,128)(2,1)S(1)} %get-tuple-element.25.refs_0_), channel_id=1, source_target_pairs={{0,16},{1,17},{2,18},{3,19},{4,20},{5,21},{6,22},{7,23},{8,24},{9,... | collective-permute-start | bytes 491528 | tf_op jit(solution)/shard_map/ppermute | solution.py:231
  15.5 0.5 %collective-permute-start.4 = (bf16[16,5120]{1,0:T(8,128)(2,1)S(1)}, bf16[16,5120]{1,0:T(8,128)(2,1)S(1)}, u32[]{:S(2)}, u32[]{:S(2)}) collective-permute-start(bf16[16,5120]{1,0:T(8,128)(2,1)S(1)} %get-tuple-element.25.refs_0_), channel_id=1, source_target_pairs={{0,8},{1,9},{2,10},{3,11},{4,12},{5,13},{6,14},{7,15},{8,0},{9,1},... | collective-permute-start | bytes 491528 | tf_op jit(solution)/shard_map/ppermute | solution.py:231
  16.1 0.0 collective-permute-start.3
  16.1 0.0 copy-start
  16.1 3.8 %shard_map.106 = (f32[200,128]{1,0:T(8,128)S(1)}, f32[4,4,128]{2,1,0:T(4,128)S(1)}, f32[4,4,128]{2,1,0:T(4,128)S(1)}, f32[128,128]{1,0:T(8,128)S(1)}) custom-call(bf16[16,1280]{1,0:T(8,128)(2,1)S(1)} %get-tuple-element.26.refs_0_, bf16[16,1280]{1,0:T(8,128)(2,1)S(1)} %collective-permute-done.refs_1_, bf16[16,1280]{1,0:T(8,128)(2,1)S(1)} %collective-permute-done.1.refs_2_, ...), custom_call_target="tpu_custom_call" | custom-call | bytes 12000000 | tf_op jit(solution)/shard_map/pallas_call | solution.py:44
  19.9 0.5 %collective-permute-done.6.refs_6_ = bf16[16,5120]{1,0:T(8,128)(2,1)S(1)} collective-permute-done((bf16[16,5120]{1,0:T(8,128)(2,1)S(1)}, bf16[16,5120]{1,0:T(8,128)(2,1)S(1)}, u32[]{:S(2)}, u32[]{:S(2)}) %collective-permute-start.6) | collective-permute-done | bytes 163872 | tf_op jit(solution)/shard_map/ppermute | solution.py:231
  20.4 1.0 %collective-permute-done.5.refs_4_ = bf16[16,5120]{1,0:T(8,128)(2,1)S(1)} collective-permute-done((bf16[16,5120]{1,0:T(8,128)(2,1)S(1)}, bf16[16,5120]{1,0:T(8,128)(2,1)S(1)}, u32[]{:S(2)}, u32[]{:S(2)}) %collective-permute-start.5) | collective-permute-done | bytes 163872 | tf_op jit(solution)/shard_map/ppermute | solution.py:231
  21.3 0.1 collective-permute-done.4.refs_2_
  21.4 0.0 copy-start.1
  21.4 0.0 copy-start.2
  21.4 0.0 collective-permute-start.7
  21.4 0.5 %collective-permute-start.8 = (bf16[16,5120]{1,0:T(8,128)(2,1)S(1)}, bf16[16,5120]{1,0:T(8,128)(2,1)S(1)}, u32[]{:S(2)}, u32[]{:S(2)}) collective-permute-start(bf16[16,5120]{1,0:T(8,128)(2,1)S(1)} %collective-permute-done.5.refs_4_), channel_id=1, source_target_pairs={{0,4},{1,5},{2,6},{3,7},{4,0},{5,1},{6,2},{7,3},{8,12},{9,13},{10,... | collective-permute-start | bytes 491528 | tf_op jit(solution)/shard_map/ppermute | solution.py:231
  21.9 0.1 collective-permute-start.9
  22.0 0.0 collective-permute-done.3.refs_1_
  22.0 0.8 %collective-permute-done.7.refs_3_ = bf16[16,5120]{1,0:T(8,128)(2,1)S(1)} collective-permute-done((bf16[16,5120]{1,0:T(8,128)(2,1)S(1)}, bf16[16,5120]{1,0:T(8,128)(2,1)S(1)}, u32[]{:S(2)}, u32[]{:S(2)}) %collective-permute-start.7) | collective-permute-done | bytes 163872 | tf_op jit(solution)/shard_map/ppermute | solution.py:231
  22.8 0.2 collective-permute-done.8.refs_5_
  23.1 0.3 collective-permute-done.9.refs_7_
  23.3 0.0 copy-done
  23.3 1.4 %shard_map.107 = bf16[32,16,128]{2,1,0:T(8,128)(2,1)S(1)} custom-call(bf16[16,5120]{1,0:T(8,128)(2,1)S(1)} %get-tuple-element.25.refs_0_, bf16[16,5120]{1,0:T(8,128)(2,1)S(1)} %collective-permute-done.3.refs_1_, bf16[16,5120]{1,0:T(8,128)(2,1)S(1)} %collective-permute-done.4.refs_2_, bf16[16,5120]{1,0:T(8,128)(2,1)S(1)} %collective-permute-done.7.refs_3_, ...), custom_call_target="tpu_custom_call" | custom-call | bytes 6000000 | tf_op jit(solution)/shard_map/pallas_call | solution.py:44
  24.7 10.6 %all_to_all.10.parts = bf16[32,16,128]{2,1,0:T(8,128)(2,1)S(1)} all-to-all(bf16[32,16,128]{2,1,0:T(8,128)(2,1)S(1)} %shard_map.107), channel_id=1, replica_groups=mesh['dp'=8,'vocab'=4] {'dp','vocab'}, dimensions={0} | all-to-all | bytes 262144 | tf_op jit(solution)/shard_map/all_to_all | solution.py:307
  35.3 0.9 %shard_map.108 = (bf16[32,8,128]{2,1,0:T(8,128)(2,1)S(1)}, f32[1,16]{1,0:T(1,128)}) custom-call(bf16[32,16,128]{2,1,0:T(8,128)(2,1)S(1)} %all_to_all.10.parts, f32[4,4,128]{2,1,0:T(4,128)S(1)} %get-tuple-element.40.hidden_projs, f32[4,4,128]{2,1,0:T(4,128)S(1)} %get-tuple-element.41.root_means), custom_call_target="tpu_custom_call" | custom-call | bytes 3000000 | tf_op jit(solution)/shard_map/pallas_call | solution.py:44
  36.2 9.2 %all_to_all.11.parts = bf16[32,8,128]{2,1,0:T(8,128)(2,1)S(1)} all-to-all(bf16[32,8,128]{2,1,0:T(8,128)(2,1)S(1)} %get-tuple-element.42), channel_id=1, replica_groups=mesh['dp'=8,'vocab'=4] {'dp','vocab'}, dimensions={0} | all-to-all | bytes 131072 | tf_op jit(solution)/shard_map/all_to_all | solution.py:313
  45.4 0.0 copy-done.1
  45.4 0.0 copy-done.2
  45.4 1.5 %shard_map.109 = f32[4,64]{1,0:T(4,128)} custom-call(bf16[32,8,128]{2,1,0:T(8,128)(2,1)S(1)} %all_to_all.11.parts, s32[1,128]{1,0:T(1,128)S(1)} %bitcast.4, bf16[64,16384]{1,0:T(8,128)(2,1)S(1)} %copy-done.1), custom_call_target="tpu_custom_call" | custom-call | bytes 3000000 | tf_op jit(solution)/shard_map/pallas_call | solution.py:44
Async XLA Ops:
  0.6 6.9 %collective-permute-start = (bf16[16,1280]{1,0:T(8,128)(2,1)}, bf16[16,1280]{1,0:T(8,128)(2,1)S(1)}, u32[]{:S(2)}, u32[]{:S(2)}) collective-permute-start(bf16[16,1280]{1,0:T(8,128)(2,1)} %hidden_hbm.1), channel_id=1, source_target_pairs={{0,2},{1,3},{2,0},{3,1},{4,6},{5,7},{6,4},{7,5},{8,10},{9,11},{10,... | collective-permute-start | bytes 122888 | tf_op jit(solution)/shard_map/ppermute | solution.py:231
  4.8 4.2 %collective-permute-start.2 = (bf16[16,1280]{1,0:T(8,128)(2,1)}, bf16[16,1280]{1,0:T(8,128)(2,1)S(1)}, u32[]{:S(2)}, u32[]{:S(2)}) collective-permute-start(bf16[16,1280]{1,0:T(8,128)(2,1)} %hidden_hbm.1), channel_id=1, source_target_pairs={{0,1},{1,0},{2,3},{3,2},{4,5},{5,4},{6,7},{7,6},{8,9},{9,8},{10,11... | collective-permute-start | bytes 122888 | tf_op jit(solution)/shard_map/ppermute | solution.py:231
  6.3 6.0 %collective-permute-start.1 = (bf16[16,1280]{1,0:T(8,128)(2,1)}, bf16[16,1280]{1,0:T(8,128)(2,1)S(1)}, u32[]{:S(2)}, u32[]{:S(2)}) collective-permute-start(bf16[16,1280]{1,0:T(8,128)(2,1)} %hidden_hbm.1), channel_id=1, source_target_pairs={{0,3},{1,2},{2,1},{3,0},{4,7},{5,6},{6,5},{7,4},{8,11},{9,10},{10,... | collective-permute-start | bytes 122888 | tf_op jit(solution)/shard_map/ppermute | solution.py:231
  12.5 7.8 %collective-permute-start.6 = (bf16[16,5120]{1,0:T(8,128)(2,1)S(1)}, bf16[16,5120]{1,0:T(8,128)(2,1)S(1)}, u32[]{:S(2)}, u32[]{:S(2)}) collective-permute-start(bf16[16,5120]{1,0:T(8,128)(2,1)S(1)} %get-tuple-element.25.refs_0_), channel_id=1, source_target_pairs={{0,24},{1,25},{2,26},{3,27},{4,28},{5,29},{6,30},{7,31},{8,16},{9,... | collective-permute-start | bytes 491528 | tf_op jit(solution)/shard_map/ppermute | solution.py:231
  15.0 6.3 %collective-permute-start.5 = (bf16[16,5120]{1,0:T(8,128)(2,1)S(1)}, bf16[16,5120]{1,0:T(8,128)(2,1)S(1)}, u32[]{:S(2)}, u32[]{:S(2)}) collective-permute-start(bf16[16,5120]{1,0:T(8,128)(2,1)S(1)} %get-tuple-element.25.refs_0_), channel_id=1, source_target_pairs={{0,16},{1,17},{2,18},{3,19},{4,20},{5,21},{6,22},{7,23},{8,24},{9,... | collective-permute-start | bytes 491528 | tf_op jit(solution)/shard_map/ppermute | solution.py:231
  15.5 5.9 %collective-permute-start.4 = (bf16[16,5120]{1,0:T(8,128)(2,1)S(1)}, bf16[16,5120]{1,0:T(8,128)(2,1)S(1)}, u32[]{:S(2)}, u32[]{:S(2)}) collective-permute-start(bf16[16,5120]{1,0:T(8,128)(2,1)S(1)} %get-tuple-element.25.refs_0_), channel_id=1, source_target_pairs={{0,8},{1,9},{2,10},{3,11},{4,12},{5,13},{6,14},{7,15},{8,0},{9,1},... | collective-permute-start | bytes 491528 | tf_op jit(solution)/shard_map/ppermute | solution.py:231
  16.1 5.9 %collective-permute-start.3 = (bf16[16,5120]{1,0:T(8,128)(2,1)S(1)}, bf16[16,5120]{1,0:T(8,128)(2,1)S(1)}, u32[]{:S(2)}, u32[]{:S(2)}) collective-permute-start(bf16[16,5120]{1,0:T(8,128)(2,1)S(1)} %get-tuple-element.25.refs_0_), channel_id=1, source_target_pairs={{0,4},{1,5},{2,6},{3,7},{4,0},{5,1},{6,2},{7,3},{8,12},{9,13},{10,... | collective-permute-start | bytes 491528 | tf_op jit(solution)/shard_map/ppermute | solution.py:231
  16.1 7.3 %copy-start = (bf16[200,5120]{1,0:T(8,128)(2,1)S(1)}, bf16[200,5120]{1,0:T(8,128)(2,1)}, u32[]{:S(2)}) copy-start(bf16[200,5120]{1,0:T(8,128)(2,1)} %refs_8_.1) | copy-start | bytes 6144004
  21.4 24.0 %copy-start.1 = (bf16[64,16384]{1,0:T(8,128)(2,1)S(1)}, bf16[64,16384]{1,0:T(8,128)(2,1)}, u32[]{:S(2)}) copy-start(bf16[64,16384]{1,0:T(8,128)(2,1)} %store.1) | copy-start | bytes 6291460
  21.4 24.0 %copy-start.2 = (s32[128]{0:T(128)S(1)}, s32[128]{0:T(128)}, u32[]{:S(2)}) copy-start(s32[128]{0:T(128)} %param.16) | copy-start | bytes 1540
  21.4 1.4 %collective-permute-start.7 = (bf16[16,5120]{1,0:T(8,128)(2,1)S(1)}, bf16[16,5120]{1,0:T(8,128)(2,1)S(1)}, u32[]{:S(2)}, u32[]{:S(2)}) collective-permute-start(bf16[16,5120]{1,0:T(8,128)(2,1)S(1)} %collective-permute-done.4.refs_2_), channel_id=1, source_target_pairs={{0,4},{1,5},{2,6},{3,7},{4,0},{5,1},{6,2},{7,3},{8,12},{9,13},{10,... | collective-permute-start | bytes 491528 | tf_op jit(solution)/shard_map/ppermute | solution.py:231
  21.4 1.6 %collective-permute-start.8 = (bf16[16,5120]{1,0:T(8,128)(2,1)S(1)}, bf16[16,5120]{1,0:T(8,128)(2,1)S(1)}, u32[]{:S(2)}, u32[]{:S(2)}) collective-permute-start(bf16[16,5120]{1,0:T(8,128)(2,1)S(1)} %collective-permute-done.5.refs_4_), channel_id=1, source_target_pairs={{0,4},{1,5},{2,6},{3,7},{4,0},{5,1},{6,2},{7,3},{8,12},{9,13},{10,... | collective-permute-start | bytes 491528 | tf_op jit(solution)/shard_map/ppermute | solution.py:231
  21.9 1.4 %collective-permute-start.9 = (bf16[16,5120]{1,0:T(8,128)(2,1)S(1)}, bf16[16,5120]{1,0:T(8,128)(2,1)S(1)}, u32[]{:S(2)}, u32[]{:S(2)}) collective-permute-start(bf16[16,5120]{1,0:T(8,128)(2,1)S(1)} %collective-permute-done.6.refs_6_), channel_id=1, source_target_pairs={{0,4},{1,5},{2,6},{3,7},{4,0},{5,1},{6,2},{7,3},{8,12},{9,13},{10,... | collective-permute-start | bytes 491528 | tf_op jit(solution)/shard_map/ppermute | solution.py:231
where the time goes:
time: 47.2 us; the launch traced here: 46.9 us
  blocking collectives  19.8 us (42%)
  starting transfers between devices  9.84 us (21%)
  Pallas kernels  8.66 us (18%)
  waiting for transfers between devices  8 us (17%)
  between operations  0.68 us (1%)
    all_to_all x1, blocking collectives, steps(): partial = lax.all_to_all(partial, AXES, 0, 0, tiled=True)  10.6 us
    ppermute x10, starting transfers between devices, swap(): return lax.ppermute(x, AXES, [(i, i ^ mask) for i in range(count)])  9.84 us
    all_to_all x1, blocking collectives, steps(): merged = lax.all_to_all(merged, AXES, 0, 0, tiled=True)  9.17 us
    pallas_call x6, Pallas kernels, placed(): run(*[pltpu.with_memory_space_constraint(x, pltpu.HBM) if i in hbm_at els...  8.66 us
    ppermute x10, waiting for transfers between devices, swap(): return lax.ppermute(x, AXES, [(i, i ^ mask) for i in range(count)])  8 us
  transfers between devices with their start and end apart: 10, of which 9 were waited for; matrix products, arithmetic and copies ran while one was open for 0% of the time, Pallas kernels for 10%

commit v1 on v0

--- a/solution.py
+++ b/solution.py
@@ -78,12 +78,12 @@
         root_mean[c] = wide_root[c * rows : (c + 1) * rows]
 
 
-def side_kernel(offsets, *refs):
+def side_kernel(offsets, others, *refs):
     n = len(offsets)
-    pieces = refs[:n]
-    sources, gain = refs[n : n + 5], refs[n + 5]
-    weights, in_part, hidden_proj, target_column = refs[n + 6 : n + 10]
-    buffers, sems = refs[n + 10 : n + 15], refs[n + 15]
+    pieces, other_unembeds, refs = refs[:n], refs[n : n + others], refs[n + others :]
+    sources, gain = refs[:5], refs[5]
+    weights, in_part, hidden_proj, target_column = refs[6:10]
+    buffers, sems = refs[10:15], refs[15]
     copies = [
         pltpu.make_async_copy(source, buffer, sems.at[i])
         for i, (source, buffer) in enumerate(zip(sources, buffers, strict=True))
@@ -97,8 +97,9 @@
         width = piece.shape[1]
         total = total + dot(piece[...], proj_out[pl.ds(pl.multiple_of(offset(), 16), width), :])
     copies[1].wait()
-    scaled_high, scaled_low = split(unembed[...].astype(F32) * gain[...])
-    weights[...] = dot(scaled_high, proj_out[...]) + dot(scaled_low, proj_out[...])
+    for u, rows_of in enumerate((unembed, *other_unembeds)):
+        scaled_high, scaled_low = split(rows_of[...].astype(F32) * gain[...])
+        weights[u] = dot(scaled_high, proj_out[...]) + dot(scaled_low, proj_out[...])
     for copy in copies[2:]:
         copy.wait()
     tokens = targets.shape[1]
@@ -112,31 +113,40 @@
         hidden_proj[c] = total[c * rows : (c + 1) * rows]
 
 
-def logits_kernel(order, *refs):
+def logits_kernel(order, twin, *refs):
     n = len(order)
-    pieces = refs[:n]
-    unembed, target_column, weights, in_part, out, placed = refs[n:]
+    pieces, unembeds = refs[:n], refs[n : n + twin]
+    target_column, weights, in_part, out, placed, placed_target = refs[n + twin :]
     rows = pieces[0].shape[0]
-    relative = dot(jnp.concatenate([piece[...] for piece in pieces], axis=0), unembed[...], ((1,), (1,)))
-    for k, token_at in enumerate(order):
-        placed[pl.ds(pl.multiple_of(token_at(), 16), rows), :] = relative[k * rows : (k + 1) * rows]
-    logits = placed[...]
-    tokens = logits.shape[0]
-    entries = logits.shape[1]
-    place = lax.axis_index("dp") * lax.axis_size("vocab") + lax.axis_index("vocab")
-    column = lax.broadcasted_iota(jnp.int32, logits.shape, 1) + place * entries
-    onehot = target_column[:, 0:1] == column.astype(F32)
-    peak = jnp.max(logits, axis=1, keepdims=True)
-    shifted = logits - peak
-    other = jnp.where(onehot, 0.0, jnp.exp(shifted))
-    total = jnp.sum(other, axis=1, keepdims=True)
-    moment = jnp.sum(other * shifted, axis=1, keepdims=True)
-    target_logit = jnp.sum(jnp.where(onehot, logits, 0.0), axis=1, keepdims=True)
-    w_high, w_low = split(weights[...])
-    p_high, p_low = split(other)
-    sums = dot(p_high, w_high) + (dot(p_high, w_low) + dot(p_low, w_high))
-    hot = onehot.astype(F32).astype(BF16)
-    target_row = dot(hot, w_high) + dot(hot, w_low)
+    normed = jnp.concatenate([piece[...] for piece in pieces], axis=0)
+    entries = unembeds[0].shape[0]
+    mine, own = lax.axis_index("dp"), lax.axis_size("vocab")
+    starts = [(pl.multiple_of(local(), 16), pl.multiple_of(whole(), 16)) for local, whole in order]
+    for local, whole in starts:
+        placed_target[pl.ds(local, rows), :] = target_column[pl.ds(whole, rows), :]
+    logits, onehot = [], []
+    for u, unembed in enumerate(unembeds):
+        relative = dot(normed, unembed[...], ((1,), (1,)))
+        for k, (local, _) in enumerate(starts):
+            placed[u, pl.ds(local, rows), :] = relative[k * rows : (k + 1) * rows]
+        logits.append(placed[u])
+        place = (mine ^ u) * own + lax.axis_index("vocab")
+        column = lax.broadcasted_iota(jnp.int32, relative.shape, 1) + place * entries
+        onehot.append(placed_target[:, 0:1] == column.astype(F32))
+    tokens = logits[0].shape[0]
+    peak = functools.reduce(jnp.maximum, [jnp.max(x, axis=1, keepdims=True) for x in logits])
+    total = moment = target_logit = sums = target_row = 0.0
+    for u in range(twin):
+        shifted = logits[u] - peak
+        other = jnp.where(onehot[u], 0.0, jnp.exp(shifted))
+        total = total + jnp.sum(other, axis=1, keepdims=True)
+        moment = moment + jnp.sum(other * shifted, axis=1, keepdims=True)
+        target_logit = target_logit + jnp.sum(jnp.where(onehot[u], logits[u], 0.0), axis=1, keepdims=True)
+        w_high, w_low = split(weights[u])
+        p_high, p_low = split(other)
+        sums = sums + (dot(p_high, w_high) + (dot(p_high, w_low) + dot(p_low, w_high)))
+        hot = onehot[u].astype(F32).astype(BF16)
+        target_row = target_row + (dot(hot, w_high) + dot(hot, w_low))
     lane = lax.broadcasted_iota(jnp.int32, (tokens, 128), 1)
     which = (lane // 2) % 4
     stats = jnp.where(which < 2, jnp.where(which == 0, peak, total), jnp.where(which == 2, moment, target_logit))
@@ -145,28 +155,29 @@
     low = stats - high - middle
     piece = (lane // 8) % 4
     stats = jnp.where(piece == 0, high, jnp.where(piece == 1, middle, jnp.where(piece == 2, low, 0.0)))
-    chunks, rows = out.shape[0], tokens // out.shape[0]
-    own = in_part.shape[0]
-    mine = lax.axis_index("dp")
+    chunks = out.shape[0]
+    rows = tokens * twin // chunks
     block = lax.broadcasted_iota(jnp.int32, (rows, 128), 1) // (128 // own)
     for d in range(chunks // own):
-        row_stats = stats[d * own * rows : (d * own + 1) * rows]
+        first = d // twin * own
+        row_stats = stats[first * rows : (first + 1) * rows]
         for k in range(1, own):
-            c = d * own + k
-            row_stats = jnp.where(block == k, stats[c * rows : (c + 1) * rows], row_stats)
+            row_stats = jnp.where(block == k, stats[(first + k) * rows : (first + k + 1) * rows], row_stats)
         for k in range(own):
-            c = d * own + k
-            here = slice(c * rows, (c + 1) * rows)
+            here = slice((first + k) * rows, (first + k + 1) * rows)
             terms = jnp.where(mine == d, in_part[k], 0.0)
-            out[c] = jnp.concatenate([sums[here], target_row[here], terms, row_stats], axis=0).astype(BF16)
+            packed = jnp.concatenate([sums[here], target_row[here], terms, row_stats], axis=0)
+            out[d * own + k] = packed.astype(BF16)
 
 
 def merge_kernel(features, parts, hidden_projs, root_means, out, logprob):
     index, own = lax.axis_index("vocab"), lax.axis_size("vocab")
     hidden_proj = hidden_projs[index]
     root_mean = root_means[index]
-    chunks, rows = parts.shape[0], hidden_proj.shape[0]
-    received = parts[...].astype(F32)
+    rows = hidden_proj.shape[0]
+    chunks = parts.shape[0] * own
+    received = parts[:, lax.axis_index("dp") % parts.shape[1]]
+    received = received.reshape(chunks, *received.shape[2:]).astype(F32)
     stats = received[:, 3 * rows : 4 * rows].reshape(chunks * rows, 128)
     stats = stats + pltpu.roll(stats, 128 - 8, 1) + pltpu.roll(stats, 128 - 16, 1)
     shape = (chunks, rows, 128)
@@ -247,6 +258,8 @@
     gain_row = gain.reshape(1, features)
 
     sds = jax.ShapeDtypeStruct
+    fast = n_dp == 8 and n_vocab == 4 and width % 128 == 0
+    twin = 2 if fast else 1
     row_shape = sds((n_vocab, per_device, projected), F32)
 
     def norm(row_pieces, offsets, gain_row):
@@ -254,20 +267,22 @@
             functools.partial(norm_kernel, offsets), (sds((rows, features), BF16), row_shape), len(row_pieces) + 1
         )(*row_pieces, gain_row)
 
-    def side_work(row_pieces, offsets, gain_row):
+    def side_work(row_pieces, offsets, others, gain_row):
         n = len(row_pieces)
         sources = (proj_out, unembed, proj_in, inputs, targets.reshape(1, tokens))
+        n += len(others)
         return call(
-            functools.partial(side_kernel, offsets),
-            (sds((entries, projected), F32), row_shape, row_shape, sds((tokens, 128), F32)),
+            functools.partial(side_kernel, offsets, len(others)),
+            (sds((twin, entries, projected), F32), row_shape, row_shape, sds((tokens, 128), F32)),
             n + 6,
             hbm_at=range(n, n + 5),
             scratch=[pltpu.VMEM(x.shape, x.dtype) for x in sources] + [pltpu.SemaphoreType.DMA((5,))],
             us=4.0,
-        )(*row_pieces, *sources, gain_row)
-
-    if n_dp == 8 and n_vocab == 4 and width % 128 == 0:
+        )(*row_pieces, *others, *sources, gain_row)
+
+    if fast:
         row_pieces = [swap(hidden, size, k) for k in (2, 3, 1)]
+        others = [swap(unembed, size, n_vocab)]
         staged, gain_row = call(
             stage_kernel,
             (sds(hidden.shape, BF16), sds(gain_row.shape, F32)),
@@ -278,33 +293,34 @@
         row_pieces = [staged] + row_pieces
         offsets = [lambda k=k: (lax.axis_index("vocab") ^ k) * width for k in (0, 2, 3, 1)]
         normed, root_mean = norm(row_pieces, offsets, gain_row)
-        near = {0: normed}
-        for r in (6, 2, 4):
-            near[r] = swap(normed, size, r * n_vocab)
         *row_pieces, _ = lax.optimization_barrier((*row_pieces, normed))
-        side = side_work(row_pieces, offsets, gain_row)
-        near[2], near[4], near[6], side = lax.optimization_barrier((near[2], near[4], near[6], side))
-        pieces = dict(near)
-        for r in (0, 6, 2, 4):
-            pieces[r + 1] = swap(near[r], size, n_vocab)
-        pieces = [pieces[r] for r in range(n_dp)]
-        order = [lambda r=r: (lax.axis_index("dp") ^ r) * rows for r in range(n_dp)]
+        side = side_work(row_pieces, offsets, others, gain_row)
+        masks = (0, 6, 4, 2)
+        pieces = [normed] + [swap(normed, size, r * n_vocab) for r in masks[1:]]
+        order = [
+            (
+                lambda r=r: (lax.axis_index("dp") ^ r) // 2 * rows,
+                lambda r=r: (lax.axis_index("dp") ^ r) * rows,
+            )
+            for r in masks
+        ]
     else:
         row_pieces = [lax.all_gather(hidden, "vocab", axis=1, tiled=True)]
-        offsets = [lambda: 0]
+        offsets, others = [lambda: 0], []
         normed, root_mean = norm(row_pieces, offsets, gain_row)
-        side = side_work(row_pieces, offsets, gain_row)
+        side = side_work(row_pieces, offsets, others, gain_row)
         pieces = [lax.all_gather(normed, "dp", axis=0, tiled=True)]
-        order = [lambda: 0]
+        order = [(lambda: 0, lambda: 0)]
     weights, in_part, hidden_proj, target_column = side
     partial = call(
-        functools.partial(logits_kernel, order),
+        functools.partial(logits_kernel, order, twin),
         sds((devices, 4 * per_device, projected), BF16),
-        len(pieces) + 4,
-        scratch=[pltpu.VMEM((tokens, entries), F32)],
+        len(pieces) + twin + 3,
+        scratch=[pltpu.VMEM((twin, tokens // twin, entries), F32), pltpu.VMEM((tokens // twin, 128), F32)],
         us=2.0,
-    )(*pieces, unembed, target_column, weights, in_part)
+    )(*pieces, unembed, *others, target_column, weights, in_part)
     partial = lax.all_to_all(partial, AXES, 0, 0, tiled=True)
+    partial = partial.reshape(n_dp // twin, twin, n_vocab, 4 * per_device, projected)
     merged, logprob = call(
         functools.partial(merge_kernel, features),
         (sds((devices, 2 * per_device, projected), BF16), sds((1, rows), F32)),

time: 47.2 us -> 47.5 us (level)
  waiting for transfers between devices: 8 us -> 4.66 us
  blocking collectives: 19.8 us -> 22.3 us
  Pallas kernels: 8.66 us -> 10.3 us
  starting transfers between devices: 9.84 us -> 9.34 us
    ppermute x10 -> x7, waiting for transfers between devices: 8 us -> 4.66 us  [swap(): return lax.ppermute(x, AXES, [(i, i ^ mask) for i in range(count)])]
    all_to_all x1, blocking collectives: 10.6 us -> 13.1 us  [steps(): partial = lax.all_to_all(partial, AXES, 0, 0, tiled=True)]
    pallas_call x6, Pallas kernels: 8.66 us -> 10.3 us  [placed(): run(*[pltpu.with_memory_space_constraint(x, pltpu.HBM) if i in hbm_at els...]
    ppermute x10 -> x7, starting transfers between devices: 9.84 us -> 9.34 us  [swap(): return lax.ppermute(x, AXES, [(i, i ^ mask) for i in range(count)])]
  transfers between devices with their start and end apart: 10 -> 7, of which waited for: 9 -> 3; matrix products, arithmetic and copies ran while one was open for 0% -> 0% of each run, Pallas kernels for 10% -> 13%
where the time goes in v1:
time: 47.5 us; the launch traced here: 47.3 us
  blocking collectives  22.3 us (47%)
  Pallas kernels  10.3 us (22%)
  starting transfers between devices  9.34 us (20%)
  waiting for transfers between devices  4.66 us (10%)
  between operations  0.69 us (1%)
    all_to_all x1, blocking collectives, steps(): partial = lax.all_to_all(partial, AXES, 0, 0, tiled=True)  13.1 us
    pallas_call x6, Pallas kernels, placed(): run(*[pltpu.with_memory_space_constraint(x, pltpu.HBM) if i in hbm_at els...  10.3 us
    ppermute x7, starting transfers between devices, swap(): return lax.ppermute(x, AXES, [(i, i ^ mask) for i in range(count)])  9.34 us
    all_to_all x1, blocking collectives, steps(): merged = lax.all_to_all(merged, AXES, 0, 0, tiled=True)  9.17 us
    ppermute x7, waiting for transfers between devices, swap(): return lax.ppermute(x, AXES, [(i, i ^ mask) for i in range(count)])  4.66 us
  transfers between devices with their start and end apart: 7, of which 3 were waited for; matrix products, arithmetic and copies ran while one was open for 0% of the time, Pallas kernels for 13%

profile of v1, /device:TPU:0, one launch (start us, length us, event | category | flops | bytes accessed | tf_op | source)
XLA Modules:
  0.0 47.3 jit_solution(1531350771516301857)
XLA Ops:
  0.6 0.6 %collective-permute-start.6 = (bf16[200,5120]{1,0:T(8,128)(2,1)}, bf16[200,5120]{1,0:T(8,128)(2,1)S(1)}, u32[]{:S(2)}, u32[]{:S(2)}) collective-permute-start(bf16[200,5120]{1,0:T(8,128)(2,1)} %refs_4_.1), channel_id=1, source_target_pairs={{0,4},{1,5},{2,6},{3,7},{4,0},{5,1},{6,2},{7,3},{8,12},{9,13},{10,... | collective-permute-start | bytes 6144008 | tf_op jit(solution)/shard_map/ppermute | solution.py:242
  1.2 3.7 %collective-permute-start = (bf16[16,1280]{1,0:T(8,128)(2,1)}, bf16[16,1280]{1,0:T(8,128)(2,1)S(1)}, u32[]{:S(2)}, u32[]{:S(2)}) collective-permute-start(bf16[16,1280]{1,0:T(8,128)(2,1)} %hidden_hbm.1), channel_id=1, source_target_pairs={{0,2},{1,3},{2,0},{3,1},{4,6},{5,7},{6,4},{7,5},{8,10},{9,11},{10,... | collective-permute-start | bytes 122888 | tf_op jit(solution)/shard_map/ppermute | solution.py:242
  4.8 1.3 %collective-permute-start.1 = (bf16[16,1280]{1,0:T(8,128)(2,1)}, bf16[16,1280]{1,0:T(8,128)(2,1)S(1)}, u32[]{:S(2)}, u32[]{:S(2)}) collective-permute-start(bf16[16,1280]{1,0:T(8,128)(2,1)} %hidden_hbm.1), channel_id=1, source_target_pairs={{0,3},{1,2},{2,1},{3,0},{4,7},{5,6},{6,5},{7,4},{8,11},{9,10},{10,... | collective-permute-start | bytes 122888 | tf_op jit(solution)/shard_map/ppermute | solution.py:242
  6.2 0.2 collective-permute-start.2
  6.4 0.8 %shard_map.104 = (bf16[16,1280]{1,0:T(8,128)(2,1)S(1)}, f32[1,5120]{1,0:T(1,128)S(1)}) custom-call(bf16[16,1280]{1,0:T(8,128)(2,1)} %hidden_hbm.1, f32[1,5120]{1,0:T(1,128)} %bitcast.7), custom_call_target="tpu_custom_call" | custom-call | bytes 3000000 | tf_op jit(solution)/shard_map/pallas_call | solution.py:44
  7.3 0.0 collective-permute-done.refs_1_
  7.3 3.6 %collective-permute-done.1.refs_2_ = bf16[16,1280]{1,0:T(8,128)(2,1)S(1)} collective-permute-done((bf16[16,1280]{1,0:T(8,128)(2,1)}, bf16[16,1280]{1,0:T(8,128)(2,1)S(1)}, u32[]{:S(2)}, u32[]{:S(2)}) %collective-permute-start.1) | collective-permute-done | bytes 40992 | tf_op jit(solution)/shard_map/ppermute | solution.py:242
  10.9 0.0 collective-permute-done.2.refs_3_
  10.9 0.2 shard_map.105
  11.1 2.5 %collective-permute-start.3 = (bf16[16,5120]{1,0:T(8,128)(2,1)S(1)}, bf16[16,5120]{1,0:T(8,128)(2,1)S(1)}, u32[]{:S(2)}, u32[]{:S(2)}) collective-permute-start(bf16[16,5120]{1,0:T(8,128)(2,1)S(1)} %get-tuple-element.18.refs_0_), channel_id=1, source_target_pairs={{0,24},{1,25},{2,26},{3,27},{4,28},{5,29},{6,30},{7,31},{8,16},{9,... | collective-permute-start | bytes 491528 | tf_op jit(solution)/shard_map/ppermute | solution.py:242
  13.6 0.5 %collective-permute-start.4 = (bf16[16,5120]{1,0:T(8,128)(2,1)S(1)}, bf16[16,5120]{1,0:T(8,128)(2,1)S(1)}, u32[]{:S(2)}, u32[]{:S(2)}) collective-permute-start(bf16[16,5120]{1,0:T(8,128)(2,1)S(1)} %get-tuple-element.18.refs_0_), channel_id=1, source_target_pairs={{0,16},{1,17},{2,18},{3,19},{4,20},{5,21},{6,22},{7,23},{8,24},{9,... | collective-permute-start | bytes 491528 | tf_op jit(solution)/shard_map/ppermute | solution.py:242
  14.1 0.5 %collective-permute-start.5 = (bf16[16,5120]{1,0:T(8,128)(2,1)S(1)}, bf16[16,5120]{1,0:T(8,128)(2,1)S(1)}, u32[]{:S(2)}, u32[]{:S(2)}) collective-permute-start(bf16[16,5120]{1,0:T(8,128)(2,1)S(1)} %get-tuple-element.18.refs_0_), channel_id=1, source_target_pairs={{0,8},{1,9},{2,10},{3,11},{4,12},{5,13},{6,14},{7,15},{8,0},{9,1},... | collective-permute-start | bytes 491528 | tf_op jit(solution)/shard_map/ppermute | solution.py:242
  14.7 0.0 collective-permute-done.6.refs_4_.refs_5_
  14.7 0.0 copy-start
  14.7 5.1 %shard_map.106 = (f32[2,200,128]{2,1,0:T(8,128)S(1)}, f32[4,4,128]{2,1,0:T(4,128)S(1)}, f32[4,4,128]{2,1,0:T(4,128)S(1)}, f32[128,128]{1,0:T(8,128)S(1)}) custom-call(bf16[16,1280]{1,0:T(8,128)(2,1)S(1)} %get-tuple-element.19.refs_0_, bf16[16,1280]{1,0:T(8,128)(2,1)S(1)} %collective-permute-done.refs_1_, ...), custom_call_target="tpu_custom_call" | custom-call | bytes 12000000 | tf_op jit(solution)/shard_map/pallas_call | solution.py:44
  19.8 0.0 collective-permute-done.3.refs_1_
  19.8 0.9 %collective-permute-done.4.refs_2_ = bf16[16,5120]{1,0:T(8,128)(2,1)S(1)} collective-permute-done((bf16[16,5120]{1,0:T(8,128)(2,1)S(1)}, bf16[16,5120]{1,0:T(8,128)(2,1)S(1)}, u32[]{:S(2)}, u32[]{:S(2)}) %collective-permute-start.4) | collective-permute-done | bytes 163872 | tf_op jit(solution)/shard_map/ppermute | solution.py:242
  20.7 0.1 collective-permute-done.5.refs_3_
  20.8 0.0 copy-done
  20.8 0.0 copy-start.1
  20.8 0.0 copy-start.2
  20.8 1.9 %shard_map.107 = bf16[32,16,128]{2,1,0:T(8,128)(2,1)S(1)} custom-call(bf16[16,5120]{1,0:T(8,128)(2,1)S(1)} %get-tuple-element.18.refs_0_, bf16[16,5120]{1,0:T(8,128)(2,1)S(1)} %collective-permute-done.3.refs_1_, bf16[16,5120]{1,0:T(8,128)(2,1)S(1)} %collective-permute-done.4.refs_2_, bf16[16,5120]{1,0:T(8,128)(2,1)S(1)} %collective-permute-done.5.refs_3_, ...), custom_call_target="tpu_custom_call" | custom-call | bytes 6000000 | tf_op jit(solution)/shard_map/pallas_call | solution.py:44
  22.7 13.1 %all_to_all.10 = bf16[32,16,128]{2,1,0:T(8,128)(2,1)S(1)} all-to-all(bf16[32,16,128]{2,1,0:T(8,128)(2,1)S(1)} %shard_map.107), channel_id=1, replica_groups=mesh['dp'=8,'vocab'=4] {'dp','vocab'}, dimensions={0} | all-to-all | bytes 262144 | tf_op jit(solution)/shard_map/all_to_all | solution.py:322
  35.8 0.8 %shard_map.108 = (bf16[32,8,128]{2,1,0:T(8,128)(2,1)S(1)}, f32[1,16]{1,0:T(1,128)}) custom-call(bf16[4,2,4,16,128]{4,3,2,1,0:T(8,128)(2,1)S(1)} %bitcast.5, f32[4,4,128]{2,1,0:T(4,128)S(1)} %get-tuple-element.26.hidden_projs, f32[4,4,128]{2,1,0:T(4,128)S(1)} %get-tuple-element.27.root_means), custom_call_target="tpu_custom_call" | custom-call | bytes 3000000 | tf_op jit(solution)/shard_map/pallas_call | solution.py:44
  36.6 9.2 %all_to_all.11.parts = bf16[32,8,128]{2,1,0:T(8,128)(2,1)S(1)} all-to-all(bf16[32,8,128]{2,1,0:T(8,128)(2,1)S(1)} %get-tuple-element.28), channel_id=1, replica_groups=mesh['dp'=8,'vocab'=4] {'dp','vocab'}, dimensions={0} | all-to-all | bytes 131072 | tf_op jit(solution)/shard_map/all_to_all | solution.py:329
  45.7 0.0 copy-done.1
  45.7 0.0 copy-done.2
  45.7 1.5 %shard_map.109 = f32[4,64]{1,0:T(4,128)} custom-call(bf16[32,8,128]{2,1,0:T(8,128)(2,1)S(1)} %all_to_all.11.parts, s32[1,128]{1,0:T(1,128)S(1)} %bitcast.6, bf16[64,16384]{1,0:T(8,128)(2,1)S(1)} %copy-done.1), custom_call_target="tpu_custom_call" | custom-call | bytes 3000000 | tf_op jit(solution)/shard_map/pallas_call | solution.py:44
Async XLA Ops:
  0.6 14.0 %collective-permute-start.6 = (bf16[200,5120]{1,0:T(8,128)(2,1)}, bf16[200,5120]{1,0:T(8,128)(2,1)S(1)}, u32[]{:S(2)}, u32[]{:S(2)}) collective-permute-start(bf16[200,5120]{1,0:T(8,128)(2,1)} %refs_4_.1), channel_id=1, source_target_pairs={{0,4},{1,5},{2,6},{3,7},{4,0},{5,1},{6,2},{7,3},{8,12},{9,13},{10,... | collective-permute-start | bytes 6144008 | tf_op jit(solution)/shard_map/ppermute | solution.py:242
  1.2 6.1 %collective-permute-start = (bf16[16,1280]{1,0:T(8,128)(2,1)}, bf16[16,1280]{1,0:T(8,128)(2,1)S(1)}, u32[]{:S(2)}, u32[]{:S(2)}) collective-permute-start(bf16[16,1280]{1,0:T(8,128)(2,1)} %hidden_hbm.1), channel_id=1, source_target_pairs={{0,2},{1,3},{2,0},{3,1},{4,6},{5,7},{6,4},{7,5},{8,10},{9,11},{10,... | collective-permute-start | bytes 122888 | tf_op jit(solution)/shard_map/ppermute | solution.py:242
  4.8 6.1 %collective-permute-start.1 = (bf16[16,1280]{1,0:T(8,128)(2,1)}, bf16[16,1280]{1,0:T(8,128)(2,1)S(1)}, u32[]{:S(2)}, u32[]{:S(2)}) collective-permute-start(bf16[16,1280]{1,0:T(8,128)(2,1)} %hidden_hbm.1), channel_id=1, source_target_pairs={{0,3},{1,2},{2,1},{3,0},{4,7},{5,6},{6,5},{7,4},{8,11},{9,10},{10,... | collective-permute-start | bytes 122888 | tf_op jit(solution)/shard_map/ppermute | solution.py:242
  6.2 4.8 %collective-permute-start.2 = (bf16[16,1280]{1,0:T(8,128)(2,1)}, bf16[16,1280]{1,0:T(8,128)(2,1)S(1)}, u32[]{:S(2)}, u32[]{:S(2)}) collective-permute-start(bf16[16,1280]{1,0:T(8,128)(2,1)} %hidden_hbm.1), channel_id=1, source_target_pairs={{0,1},{1,0},{2,3},{3,2},{4,5},{5,4},{6,7},{7,6},{8,9},{9,8},{10,11... | collective-permute-start | bytes 122888 | tf_op jit(solution)/shard_map/ppermute | solution.py:242
  11.1 8.7 %collective-permute-start.3 = (bf16[16,5120]{1,0:T(8,128)(2,1)S(1)}, bf16[16,5120]{1,0:T(8,128)(2,1)S(1)}, u32[]{:S(2)}, u32[]{:S(2)}) collective-permute-start(bf16[16,5120]{1,0:T(8,128)(2,1)S(1)} %get-tuple-element.18.refs_0_), channel_id=1, source_target_pairs={{0,24},{1,25},{2,26},{3,27},{4,28},{5,29},{6,30},{7,31},{8,16},{9,... | collective-permute-start | bytes 491528 | tf_op jit(solution)/shard_map/ppermute | solution.py:242
  13.6 7.1 %collective-permute-start.4 = (bf16[16,5120]{1,0:T(8,128)(2,1)S(1)}, bf16[16,5120]{1,0:T(8,128)(2,1)S(1)}, u32[]{:S(2)}, u32[]{:S(2)}) collective-permute-start(bf16[16,5120]{1,0:T(8,128)(2,1)S(1)} %get-tuple-element.18.refs_0_), channel_id=1, source_target_pairs={{0,16},{1,17},{2,18},{3,19},{4,20},{5,21},{6,22},{7,23},{8,24},{9,... | collective-permute-start | bytes 491528 | tf_op jit(solution)/shard_map/ppermute | solution.py:242
  14.1 6.7 %collective-permute-start.5 = (bf16[16,5120]{1,0:T(8,128)(2,1)S(1)}, bf16[16,5120]{1,0:T(8,128)(2,1)S(1)}, u32[]{:S(2)}, u32[]{:S(2)}) collective-permute-start(bf16[16,5120]{1,0:T(8,128)(2,1)S(1)} %get-tuple-element.18.refs_0_), channel_id=1, source_target_pairs={{0,8},{1,9},{2,10},{3,11},{4,12},{5,13},{6,14},{7,15},{8,0},{9,1},... | collective-permute-start | bytes 491528 | tf_op jit(solution)/shard_map/ppermute | solution.py:242
  14.7 6.1 %copy-start = (bf16[200,5120]{1,0:T(8,128)(2,1)S(1)}, bf16[200,5120]{1,0:T(8,128)(2,1)}, u32[]{:S(2)}) copy-start(bf16[200,5120]{1,0:T(8,128)(2,1)} %refs_4_.1) | copy-start | bytes 6144004
  20.8 24.9 %copy-start.1 = (bf16[64,16384]{1,0:T(8,128)(2,1)S(1)}, bf16[64,16384]{1,0:T(8,128)(2,1)}, u32[]{:S(2)}) copy-start(bf16[64,16384]{1,0:T(8,128)(2,1)} %store.1) | copy-start | bytes 6291460
  20.8 24.9 %copy-start.2 = (s32[128]{0:T(128)S(1)}, s32[128]{0:T(128)}, u32[]{:S(2)}) copy-start(s32[128]{0:T(128)} %param.16) | copy-start | bytes 1540

commit v2 on v1

--- a/solution.py
+++ b/solution.py
@@ -48,11 +48,15 @@
     return placed
 
 
-def stage_kernel(hidden_hbm, gain_hbm, hidden, gain, sems):
-    copies = [
-        pltpu.make_async_copy(hidden_hbm, hidden, sems.at[0]),
-        pltpu.make_async_copy(gain_hbm, gain, sems.at[1]),
-    ]
+def stage_kernel(*refs):
+    n = len(refs) // 2
+    sources, targets, sems = refs[:n], refs[n : 2 * n], refs[2 * n]
+    copies = []
+    for i, (source, target) in enumerate(zip(sources, targets, strict=True)):
+        if source.shape != target.shape:
+            width = target.shape[0]
+            source = source.at[pl.ds(pl.multiple_of(lax.axis_index("vocab") * width, 16), width), :]
+        copies.append(pltpu.make_async_copy(source, target, sems.at[i]))
     for copy in copies:
         copy.start()
     for copy in copies:
@@ -81,32 +85,17 @@
 def side_kernel(offsets, others, *refs):
     n = len(offsets)
     pieces, other_unembeds, refs = refs[:n], refs[n : n + others], refs[n + others :]
-    sources, gain = refs[:5], refs[5]
-    weights, in_part, hidden_proj, target_column = refs[6:10]
-    buffers, sems = refs[10:15], refs[15]
-    copies = [
-        pltpu.make_async_copy(source, buffer, sems.at[i])
-        for i, (source, buffer) in enumerate(zip(sources, buffers, strict=True))
-    ]
-    for copy in copies:
-        copy.start()
-    proj_out, unembed, proj_in, inputs, targets = buffers
-    copies[0].wait()
+    proj_out, unembed, proj_slice, inputs, targets, gain, weights, in_part, hidden_proj, target_column = refs
     total = 0.0
     for piece, offset in zip(pieces, offsets, strict=True):
         width = piece.shape[1]
         total = total + dot(piece[...], proj_out[pl.ds(pl.multiple_of(offset(), 16), width), :])
-    copies[1].wait()
     for u, rows_of in enumerate((unembed, *other_unembeds)):
         scaled_high, scaled_low = split(rows_of[...].astype(F32) * gain[...])
         weights[u] = dot(scaled_high, proj_out[...]) + dot(scaled_low, proj_out[...])
-    for copy in copies[2:]:
-        copy.wait()
     tokens = targets.shape[1]
     target_column[...] = jnp.broadcast_to(targets[...].astype(F32), (128, tokens)).T
-    width = inputs.shape[1]
-    start = pl.multiple_of(lax.axis_index("vocab") * width, 16)
-    part = dot(inputs[...], proj_in[pl.ds(start, width), :])
+    part = dot(inputs[...], proj_slice[...])
     chunks, rows, _ = in_part.shape
     for c in range(chunks):
         in_part[c] = part[c * rows : (c + 1) * rows]
@@ -126,7 +115,7 @@
         placed_target[pl.ds(local, rows), :] = target_column[pl.ds(whole, rows), :]
     logits, onehot = [], []
     for u, unembed in enumerate(unembeds):
-        relative = dot(normed, unembed[...], ((1,), (1,)))
+        relative = dot(unembed[...], normed, ((1,), (1,))).T
         for k, (local, _) in enumerate(starts):
             placed[u, pl.ds(local, rows), :] = relative[k * rows : (k + 1) * rows]
         logits.append(placed[u])
@@ -146,7 +135,7 @@
         p_high, p_low = split(other)
         sums = sums + (dot(p_high, w_high) + (dot(p_high, w_low) + dot(p_low, w_high)))
         hot = onehot[u].astype(F32).astype(BF16)
-        target_row = target_row + (dot(hot, w_high) + dot(hot, w_low))
+        target_row = target_row + dot(hot, w_high)
     lane = lax.broadcasted_iota(jnp.int32, (tokens, 128), 1)
     which = (lane // 2) % 4
     stats = jnp.where(which < 2, jnp.where(which == 0, peak, total), jnp.where(which == 2, moment, target_logit))
@@ -215,7 +204,8 @@
     out[...] = jnp.broadcast_to(both[None], out.shape)
 
 
-def scores_kernel(parts, segments, store, scores, out_grad, in_proj, spread, flat):
+def scores_kernel(parts, segments, store, logprob_in, scores, logprob, out_grad, in_proj, spread, flat):
+    logprob[...] = logprob_in[...]
     chunks, rows = parts.shape[0], parts.shape[1] // 2
     for c in range(chunks):
         both = parts[c].astype(F32)
@@ -262,39 +252,38 @@
     twin = 2 if fast else 1
     row_shape = sds((n_vocab, per_device, projected), F32)
 
-    def norm(row_pieces, offsets, gain_row):
+    def norm(row_pieces, offsets):
         return call(
             functools.partial(norm_kernel, offsets), (sds((rows, features), BF16), row_shape), len(row_pieces) + 1
         )(*row_pieces, gain_row)
 
-    def side_work(row_pieces, offsets, others, gain_row):
-        n = len(row_pieces)
-        sources = (proj_out, unembed, proj_in, inputs, targets.reshape(1, tokens))
-        n += len(others)
+    sources = (hidden, gain_row, proj_out, unembed, proj_in, inputs, targets.reshape(1, tokens))
+    shapes = [sds(x.shape, x.dtype) for x in sources]
+    shapes[4] = sds((inputs.shape[1], projected), BF16)
+    hidden_here, gain_row, proj_out, unembed_here, proj_slice, inputs, target_row = call(
+        stage_kernel,
+        tuple(shapes),
+        len(sources),
+        hbm_at=range(len(sources)),
+        scratch=[pltpu.SemaphoreType.DMA((len(sources),))],
+    )(*sources)
+
+    def side_work(row_pieces, offsets, others):
         return call(
             functools.partial(side_kernel, offsets, len(others)),
             (sds((twin, entries, projected), F32), row_shape, row_shape, sds((tokens, 128), F32)),
-            n + 6,
-            hbm_at=range(n, n + 5),
-            scratch=[pltpu.VMEM(x.shape, x.dtype) for x in sources] + [pltpu.SemaphoreType.DMA((5,))],
+            len(row_pieces) + len(others) + 6,
             us=4.0,
-        )(*row_pieces, *others, *sources, gain_row)
+        )(*row_pieces, *others, proj_out, unembed_here, proj_slice, inputs, target_row, gain_row)
 
     if fast:
         row_pieces = [swap(hidden, size, k) for k in (2, 3, 1)]
         others = [swap(unembed, size, n_vocab)]
-        staged, gain_row = call(
-            stage_kernel,
-            (sds(hidden.shape, BF16), sds(gain_row.shape, F32)),
-            2,
-            hbm_at=(0, 1),
-            scratch=[pltpu.SemaphoreType.DMA((2,))],
-        )(hidden, gain_row)
-        row_pieces = [staged] + row_pieces
+        row_pieces = [hidden_here] + row_pieces
         offsets = [lambda k=k: (lax.axis_index("vocab") ^ k) * width for k in (0, 2, 3, 1)]
-        normed, root_mean = norm(row_pieces, offsets, gain_row)
+        normed, root_mean = norm(row_pieces, offsets)
         *row_pieces, _ = lax.optimization_barrier((*row_pieces, normed))
-        side = side_work(row_pieces, offsets, others, gain_row)
+        side = side_work(row_pieces, offsets, others)
         masks = (0, 6, 4, 2)
         pieces = [normed] + [swap(normed, size, r * n_vocab) for r in masks[1:]]
         order = [
@@ -307,8 +296,8 @@
     else:
         row_pieces = [lax.all_gather(hidden, "vocab", axis=1, tiled=True)]
         offsets, others = [lambda: 0], []
-        normed, root_mean = norm(row_pieces, offsets, gain_row)
-        side = side_work(row_pieces, offsets, others, gain_row)
+        normed, root_mean = norm(row_pieces, offsets)
+        side = side_work(row_pieces, offsets, others)
         pieces = [lax.all_gather(normed, "dp", axis=0, tiled=True)]
         order = [(lambda: 0, lambda: 0)]
     weights, in_part, hidden_proj, target_column = side
@@ -318,7 +307,7 @@
         len(pieces) + twin + 3,
         scratch=[pltpu.VMEM((twin, tokens // twin, entries), F32), pltpu.VMEM((tokens // twin, 128), F32)],
         us=2.0,
-    )(*pieces, unembed, *others, target_column, weights, in_part)
+    )(*pieces, unembed_here, *others, target_column, weights, in_part)
     partial = lax.all_to_all(partial, AXES, 0, 0, tiled=True)
     partial = partial.reshape(n_dp // twin, twin, n_vocab, 4 * per_device, projected)
     merged, logprob = call(
@@ -328,17 +317,17 @@
     )(partial, hidden_proj, root_mean)
     merged = lax.all_to_all(merged, AXES, 0, 0, tiled=True)
     padded = -(-seqs // 8) * 8
-    scores = call(
+    scores, logprob = call(
         scores_kernel,
-        sds((seqs, store.shape[0]), F32),
-        3,
+        (sds((seqs, store.shape[0]), F32), sds((1, rows), F32)),
+        4,
         scratch=(
             pltpu.VMEM((tokens, projected), F32),
             pltpu.VMEM((tokens, projected), F32),
             pltpu.VMEM((projected * padded, tokens), F32),
             pltpu.VMEM((padded, store.shape[1]), F32),
         ),
-    )(merged, segment_ids.reshape(1, tokens), store)
+    )(merged, segment_ids.reshape(1, tokens), store, logprob)
     return scores, logprob.reshape(rows)
 
 

time: 47.5 us -> 46.1 us (0.971)
  waiting for transfers between devices: 4.66 us -> 7.52 us
  blocking collectives: 22.3 us -> 19.5 us
  Pallas kernels: 10.3 us -> 8.93 us
    ppermute x7, waiting for transfers between devices: 4.66 us -> 7.52 us  [swap(): return lax.ppermute(x, AXES, [(i, i ^ mask) for i in range(count)])]
    all_to_all x1, blocking collectives: 13.1 us -> 10.3 us  [steps(): partial = lax.all_to_all(partial, AXES, 0, 0, tiled=True)]
    pallas_call x6, Pallas kernels: 10.3 us -> 8.93 us  [placed(): run(*[pltpu.with_memory_space_constraint(x, pltpu.HBM) if i in hbm_at els...]
  transfers between devices with their start and end apart: 7 -> 7, of which waited for: 3 -> 4; matrix products, arithmetic and copies ran while one was open for 0% -> 0% of each run, Pallas kernels for 13% -> 11%
where the time goes in v2:
time: 46.1 us; the launch traced here: 46 us
  blocking collectives  19.5 us (42%)
  starting transfers between devices  9.34 us (20%)
  Pallas kernels  8.93 us (19%)
  waiting for transfers between devices  7.52 us (16%)
  between operations  0.68 us (1%)
    all_to_all x1, blocking collectives, steps(): partial = lax.all_to_all(partial, AXES, 0, 0, tiled=True)  10.3 us
    ppermute x7, starting transfers between devices, swap(): return lax.ppermute(x, AXES, [(i, i ^ mask) for i in range(count)])  9.34 us
    all_to_all x1, blocking collectives, steps(): merged = lax.all_to_all(merged, AXES, 0, 0, tiled=True)  9.19 us
    pallas_call x6, Pallas kernels, placed(): run(*[pltpu.with_memory_space_constraint(x, pltpu.HBM) if i in hbm_at els...  8.93 us
    ppermute x7, waiting for transfers between devices, swap(): return lax.ppermute(x, AXES, [(i, i ^ mask) for i in range(count)])  7.52 us
  transfers between devices with their start and end apart: 7, of which 4 were waited for; matrix products, arithmetic and copies ran while one was open for 0% of the time, Pallas kernels for 11%

profile of v2, /device:TPU:0, one launch (start us, length us, event | category | flops | bytes accessed | tf_op | source)
XLA Modules:
  0.0 46.0 jit_solution(5656869150717645797)
XLA Ops:
  0.6 0.6 %collective-permute-start.6 = (bf16[200,5120]{1,0:T(8,128)(2,1)}, bf16[200,5120]{1,0:T(8,128)(2,1)S(1)}, u32[]{:S(2)}, u32[]{:S(2)}) collective-permute-start(bf16[200,5120]{1,0:T(8,128)(2,1)} %refs_3_.1), channel_id=1, source_target_pairs={{0,4},{1,5},{2,6},{3,7},{4,0},{5,1},{6,2},{7,3},{8,12},{9,13},{10,... | collective-permute-start | bytes 6144008 | tf_op jit(solution)/shard_map/ppermute | solution.py:232
  1.2 3.6 %collective-permute-start = (bf16[16,1280]{1,0:T(8,128)(2,1)}, bf16[16,1280]{1,0:T(8,128)(2,1)S(1)}, u32[]{:S(2)}, u32[]{:S(2)}) collective-permute-start(bf16[16,1280]{1,0:T(8,128)(2,1)} %refs_0_.1), channel_id=1, source_target_pairs={{0,2},{1,3},{2,0},{3,1},{4,6},{5,7},{6,4},{7,5},{8,10},{9,11},{10,... | collective-permute-start | bytes 122888 | tf_op jit(solution)/shard_map/ppermute | solution.py:232
  4.8 1.6 %collective-permute-start.2 = (bf16[16,1280]{1,0:T(8,128)(2,1)}, bf16[16,1280]{1,0:T(8,128)(2,1)S(1)}, u32[]{:S(2)}, u32[]{:S(2)}) collective-permute-start(bf16[16,1280]{1,0:T(8,128)(2,1)} %refs_0_.1), channel_id=1, source_target_pairs={{0,1},{1,0},{2,3},{3,2},{4,5},{5,4},{6,7},{7,6},{8,9},{9,8},{10,11... | collective-permute-start | bytes 122888 | tf_op jit(solution)/shard_map/ppermute | solution.py:232
  6.4 0.0 collective-permute-start.1
  6.4 2.1 %shard_map.104 = (bf16[16,1280]{1,0:T(8,128)(2,1)S(1)}, f32[1,5120]{1,0:T(1,128)S(1)}, bf16[5120,128]{1,0:T(8,128)(2,1)S(1)}, bf16[200,5120]{1,0:T(8,128)(2,1)S(...) custom-call(bf16[16,1280]{1,0:T(8,128)(2,1)} %refs_0_.1, f32[1,5120]{1,0:T(1,128)} %bitcast.7, ...), custom_call_target="tpu_custom_call" | custom-call | bytes 3000000 | tf_op jit(solution)/shard_map/pallas_call | solution.py:44
  8.5 0.0 collective-permute-done.refs_1_
  8.5 0.5 %collective-permute-done.2.refs_3_ = bf16[16,1280]{1,0:T(8,128)(2,1)S(1)} collective-permute-done((bf16[16,1280]{1,0:T(8,128)(2,1)}, bf16[16,1280]{1,0:T(8,128)(2,1)S(1)}, u32[]{:S(2)}, u32[]{:S(2)}) %collective-permute-start.2) | collective-permute-done | bytes 40992 | tf_op jit(solution)/shard_map/ppermute | solution.py:232
  9.1 3.4 %collective-permute-done.1.refs_2_ = bf16[16,1280]{1,0:T(8,128)(2,1)S(1)} collective-permute-done((bf16[16,1280]{1,0:T(8,128)(2,1)}, bf16[16,1280]{1,0:T(8,128)(2,1)S(1)}, u32[]{:S(2)}, u32[]{:S(2)}) %collective-permute-start.1) | collective-permute-done | bytes 40992 | tf_op jit(solution)/shard_map/ppermute | solution.py:232
  12.4 0.2 shard_map.105
  12.6 1.6 %collective-permute-start.5 = (bf16[16,5120]{1,0:T(8,128)(2,1)S(1)}, bf16[16,5120]{1,0:T(8,128)(2,1)S(1)}, u32[]{:S(2)}, u32[]{:S(2)}) collective-permute-start(bf16[16,5120]{1,0:T(8,128)(2,1)S(1)} %get-tuple-element.25.refs_0_), channel_id=1, source_target_pairs={{0,8},{1,9},{2,10},{3,11},{4,12},{5,13},{6,14},{7,15},{8,0},{9,1},... | collective-permute-start | bytes 491528 | tf_op jit(solution)/shard_map/ppermute | solution.py:232
  14.2 1.5 %collective-permute-start.4 = (bf16[16,5120]{1,0:T(8,128)(2,1)S(1)}, bf16[16,5120]{1,0:T(8,128)(2,1)S(1)}, u32[]{:S(2)}, u32[]{:S(2)}) collective-permute-start(bf16[16,5120]{1,0:T(8,128)(2,1)S(1)} %get-tuple-element.25.refs_0_), channel_id=1, source_target_pairs={{0,16},{1,17},{2,18},{3,19},{4,20},{5,21},{6,22},{7,23},{8,24},{9,... | collective-permute-start | bytes 491528 | tf_op jit(solution)/shard_map/ppermute | solution.py:232
  15.7 0.5 %collective-permute-start.3 = (bf16[16,5120]{1,0:T(8,128)(2,1)S(1)}, bf16[16,5120]{1,0:T(8,128)(2,1)S(1)}, u32[]{:S(2)}, u32[]{:S(2)}) collective-permute-start(bf16[16,5120]{1,0:T(8,128)(2,1)S(1)} %get-tuple-element.25.refs_0_), channel_id=1, source_target_pairs={{0,24},{1,25},{2,26},{3,27},{4,28},{5,29},{6,30},{7,31},{8,16},{9,... | collective-permute-start | bytes 491528 | tf_op jit(solution)/shard_map/ppermute | solution.py:232
  16.2 0.0 collective-permute-done.6.refs_4_.refs_5_
  16.2 3.0 %shard_map.106 = (f32[2,200,128]{2,1,0:T(8,128)S(1)}, f32[4,4,128]{2,1,0:T(4,128)S(1)}, f32[4,4,128]{2,1,0:T(4,128)S(1)}, f32[128,128]{1,0:T(8,128)S(1)}) custom-call(bf16[16,1280]{1,0:T(8,128)(2,1)S(1)} %get-tuple-element.27.refs_0_, bf16[16,1280]{1,0:T(8,128)(2,1)S(1)} %collective-permute-done.refs_1_, ...), custom_call_target="tpu_custom_call" | custom-call | bytes 12000000 | tf_op jit(solution)/shard_map/pallas_call | solution.py:44
  19.2 0.4 collective-permute-done.5.refs_3_
  19.6 3.2 %collective-permute-done.4.refs_2_ = bf16[16,5120]{1,0:T(8,128)(2,1)S(1)} collective-permute-done((bf16[16,5120]{1,0:T(8,128)(2,1)S(1)}, bf16[16,5120]{1,0:T(8,128)(2,1)S(1)}, u32[]{:S(2)}, u32[]{:S(2)}) %collective-permute-start.4) | collective-permute-done | bytes 163872 | tf_op jit(solution)/shard_map/ppermute | solution.py:232
  22.8 0.0 collective-permute-done.3.refs_1_
  22.8 0.0 copy-start
  22.8 0.0 copy-start.1
  22.8 1.8 %shard_map.107 = bf16[32,16,128]{2,1,0:T(8,128)(2,1)S(1)} custom-call(bf16[16,5120]{1,0:T(8,128)(2,1)S(1)} %get-tuple-element.25.refs_0_, bf16[16,5120]{1,0:T(8,128)(2,1)S(1)} %collective-permute-done.3.refs_1_, bf16[16,5120]{1,0:T(8,128)(2,1)S(1)} %collective-permute-done.4.refs_2_, bf16[16,5120]{1,0:T(8,128)(2,1)S(1)} %collective-permute-done.5.refs_3_, ...), custom_call_target="tpu_custom_call" | custom-call | bytes 6000000 | tf_op jit(solution)/shard_map/pallas_call | solution.py:44
  24.6 10.3 %all_to_all.10 = bf16[32,16,128]{2,1,0:T(8,128)(2,1)S(1)} all-to-all(bf16[32,16,128]{2,1,0:T(8,128)(2,1)S(1)} %shard_map.107), channel_id=1, replica_groups=mesh['dp'=8,'vocab'=4] {'dp','vocab'}, dimensions={0} | all-to-all | bytes 262144 | tf_op jit(solution)/shard_map/all_to_all | solution.py:311
  34.9 0.3 shard_map.108
  35.2 9.2 %all_to_all.11.parts = bf16[32,8,128]{2,1,0:T(8,128)(2,1)S(1)} all-to-all(bf16[32,8,128]{2,1,0:T(8,128)(2,1)S(1)} %get-tuple-element.40), channel_id=1, replica_groups=mesh['dp'=8,'vocab'=4] {'dp','vocab'}, dimensions={0} | all-to-all | bytes 131072 | tf_op jit(solution)/shard_map/all_to_all | solution.py:318
  44.4 0.0 copy-done
  44.4 0.0 copy-done.1
  44.4 1.5 %shard_map.109 = (f32[4,64]{1,0:T(4,128)}, f32[1,16]{1,0:T(1,128)}) custom-call(bf16[32,8,128]{2,1,0:T(8,128)(2,1)S(1)} %all_to_all.11.parts, s32[1,128]{1,0:T(1,128)S(1)} %bitcast.6, bf16[64,16384]{1,0:T(8,128)(2,1)S(1)} %copy-done, f32[1,16]{1,0:T(1,128)S(1)} %get-tuple-element.41.logprob_in), custom_call_target="tpu_custom_call" | custom-call | bytes 3000000 | tf_op jit(solution)/shard_map/pallas_call | solution.py:44
Async XLA Ops:
  0.6 15.5 %collective-permute-start.6 = (bf16[200,5120]{1,0:T(8,128)(2,1)}, bf16[200,5120]{1,0:T(8,128)(2,1)S(1)}, u32[]{:S(2)}, u32[]{:S(2)}) collective-permute-start(bf16[200,5120]{1,0:T(8,128)(2,1)} %refs_3_.1), channel_id=1, source_target_pairs={{0,4},{1,5},{2,6},{3,7},{4,0},{5,1},{6,2},{7,3},{8,12},{9,13},{10,... | collective-permute-start | bytes 6144008 | tf_op jit(solution)/shard_map/ppermute | solution.py:232
  1.2 7.3 %collective-permute-start = (bf16[16,1280]{1,0:T(8,128)(2,1)}, bf16[16,1280]{1,0:T(8,128)(2,1)S(1)}, u32[]{:S(2)}, u32[]{:S(2)}) collective-permute-start(bf16[16,1280]{1,0:T(8,128)(2,1)} %refs_0_.1), channel_id=1, source_target_pairs={{0,2},{1,3},{2,0},{3,1},{4,6},{5,7},{6,4},{7,5},{8,10},{9,11},{10,... | collective-permute-start | bytes 122888 | tf_op jit(solution)/shard_map/ppermute | solution.py:232
  4.8 4.2 %collective-permute-start.2 = (bf16[16,1280]{1,0:T(8,128)(2,1)}, bf16[16,1280]{1,0:T(8,128)(2,1)S(1)}, u32[]{:S(2)}, u32[]{:S(2)}) collective-permute-start(bf16[16,1280]{1,0:T(8,128)(2,1)} %refs_0_.1), channel_id=1, source_target_pairs={{0,1},{1,0},{2,3},{3,2},{4,5},{5,4},{6,7},{7,6},{8,9},{9,8},{10,11... | collective-permute-start | bytes 122888 | tf_op jit(solution)/shard_map/ppermute | solution.py:232
  6.4 6.0 %collective-permute-start.1 = (bf16[16,1280]{1,0:T(8,128)(2,1)}, bf16[16,1280]{1,0:T(8,128)(2,1)S(1)}, u32[]{:S(2)}, u32[]{:S(2)}) collective-permute-start(bf16[16,1280]{1,0:T(8,128)(2,1)} %refs_0_.1), channel_id=1, source_target_pairs={{0,3},{1,2},{2,1},{3,0},{4,7},{5,6},{6,5},{7,4},{8,11},{9,10},{10,... | collective-permute-start | bytes 122888 | tf_op jit(solution)/shard_map/ppermute | solution.py:232
  12.6 7.0 %collective-permute-start.5 = (bf16[16,5120]{1,0:T(8,128)(2,1)S(1)}, bf16[16,5120]{1,0:T(8,128)(2,1)S(1)}, u32[]{:S(2)}, u32[]{:S(2)}) collective-permute-start(bf16[16,5120]{1,0:T(8,128)(2,1)S(1)} %get-tuple-element.25.refs_0_), channel_id=1, source_target_pairs={{0,8},{1,9},{2,10},{3,11},{4,12},{5,13},{6,14},{7,15},{8,0},{9,1},... | collective-permute-start | bytes 491528 | tf_op jit(solution)/shard_map/ppermute | solution.py:232
  14.2 8.6 %collective-permute-start.4 = (bf16[16,5120]{1,0:T(8,128)(2,1)S(1)}, bf16[16,5120]{1,0:T(8,128)(2,1)S(1)}, u32[]{:S(2)}, u32[]{:S(2)}) collective-permute-start(bf16[16,5120]{1,0:T(8,128)(2,1)S(1)} %get-tuple-element.25.refs_0_), channel_id=1, source_target_pairs={{0,16},{1,17},{2,18},{3,19},{4,20},{5,21},{6,22},{7,23},{8,24},{9,... | collective-permute-start | bytes 491528 | tf_op jit(solution)/shard_map/ppermute | solution.py:232
  15.7 7.1 %collective-permute-start.3 = (bf16[16,5120]{1,0:T(8,128)(2,1)S(1)}, bf16[16,5120]{1,0:T(8,128)(2,1)S(1)}, u32[]{:S(2)}, u32[]{:S(2)}) collective-permute-start(bf16[16,5120]{1,0:T(8,128)(2,1)S(1)} %get-tuple-element.25.refs_0_), channel_id=1, source_target_pairs={{0,24},{1,25},{2,26},{3,27},{4,28},{5,29},{6,30},{7,31},{8,16},{9,... | collective-permute-start | bytes 491528 | tf_op jit(solution)/shard_map/ppermute | solution.py:232
  22.8 21.6 %copy-start = (bf16[64,16384]{1,0:T(8,128)(2,1)S(1)}, bf16[64,16384]{1,0:T(8,128)(2,1)}, u32[]{:S(2)}) copy-start(bf16[64,16384]{1,0:T(8,128)(2,1)} %store.1) | copy-start | bytes 6291460
  22.8 21.6 %copy-start.1 = (s32[128]{0:T(128)S(1)}, s32[128]{0:T(128)}, u32[]{:S(2)}) copy-start(s32[128]{0:T(128)} %param.16) | copy-start | bytes 1540

commit v3 on v2

--- a/solution.py
+++ b/solution.py
@@ -51,12 +51,10 @@
 def stage_kernel(*refs):
     n = len(refs) // 2
     sources, targets, sems = refs[:n], refs[n : 2 * n], refs[2 * n]
-    copies = []
-    for i, (source, target) in enumerate(zip(sources, targets, strict=True)):
-        if source.shape != target.shape:
-            width = target.shape[0]
-            source = source.at[pl.ds(pl.multiple_of(lax.axis_index("vocab") * width, 16), width), :]
-        copies.append(pltpu.make_async_copy(source, target, sems.at[i]))
+    copies = [
+        pltpu.make_async_copy(source, target, sems.at[i])
+        for i, (source, target) in enumerate(zip(sources, targets, strict=True))
+    ]
     for copy in copies:
         copy.start()
     for copy in copies:
@@ -64,7 +62,8 @@
 
 
 def norm_kernel(offsets, *refs):
-    pieces, gain, normed, root_mean = refs[:-3], refs[-3], refs[-2], refs[-1]
+    n = len(offsets)
+    pieces, gain, root_mean, own, rest = refs[:n], refs[n], refs[n + 1], refs[n + 2], refs[n + 3 :]
     squares, features = 0.0, 0
     for piece in pieces:
         wide = piece[...].astype(F32)
@@ -72,10 +71,23 @@
         features += wide.shape[1]
     root = jnp.sqrt(squares / features + EPSILON)
     inverse = 1.0 / root
-    for piece, offset in zip(pieces, offsets, strict=True):
+    for k, (piece, offset) in enumerate(zip(pieces, offsets, strict=True)):
         width = piece.shape[1]
         here = pl.ds(pl.multiple_of(offset(), 128), width)
-        normed[:, here] = (piece[...].astype(F32) * gain[:, here] * inverse).astype(BF16)
+        value = (piece[...].astype(F32) * gain[:, here] * inverse).astype(BF16)
+        if k:
+            for target in rest:
+                target[:, (k - 1) * width : k * width] = value
+        else:
+            own[...] = value
+            if rest:
+                rest[1][:, -width:] = value
+    if rest:
+        lane = lax.broadcasted_iota(jnp.int32, (root.shape[0], 128), 1)
+        high = inverse.astype(BF16).astype(F32)
+        middle = (inverse - high).astype(BF16).astype(F32)
+        low = inverse - high - middle
+        rest[0][:, -128:] = jnp.where(lane < 32, high, jnp.where(lane < 64, middle, low)).astype(BF16)
     wide_root = jnp.broadcast_to(root, (root.shape[0], 128))
     chunks, rows, _ = root_mean.shape
     for c in range(chunks):
@@ -85,14 +97,28 @@
 def side_kernel(offsets, others, *refs):
     n = len(offsets)
     pieces, other_unembeds, refs = refs[:n], refs[n : n + others], refs[n + others :]
-    proj_out, unembed, proj_slice, inputs, targets, gain, weights, in_part, hidden_proj, target_column = refs
+    sources, gain = refs[:5], refs[5]
+    weights, in_part, hidden_proj, target_column = refs[6:10]
+    buffers, sems = refs[10:15], refs[15]
+    copies = []
+    for i, (source, buffer) in enumerate(zip(sources, buffers, strict=True)):
+        if source.shape != buffer.shape:
+            width = buffer.shape[0]
+            source = source.at[pl.ds(pl.multiple_of(lax.axis_index("vocab") * width, 16), width), :]
+        copies.append(pltpu.make_async_copy(source, buffer, sems.at[i]))
+        copies[-1].start()
+    proj_out, unembed, proj_slice, inputs, targets = buffers
+    copies[0].wait()
     total = 0.0
     for piece, offset in zip(pieces, offsets, strict=True):
         width = piece.shape[1]
         total = total + dot(piece[...], proj_out[pl.ds(pl.multiple_of(offset(), 16), width), :])
-    for u, rows_of in enumerate((unembed, *other_unembeds)):
-        scaled_high, scaled_low = split(rows_of[...].astype(F32) * gain[...])
-        weights[u] = dot(scaled_high, proj_out[...]) + dot(scaled_low, proj_out[...])
+    for u, rows_of in reversed(list(enumerate((unembed, *other_unembeds)))):
+        if u == 0:
+            copies[1].wait()
+        weights[u] = dot((rows_of[...].astype(F32) * gain[...]).astype(BF16), proj_out[...])
+    for copy in copies[2:]:
+        copy.wait()
     tokens = targets.shape[1]
     target_column[...] = jnp.broadcast_to(targets[...].astype(F32), (128, tokens)).T
     part = dot(inputs[...], proj_slice[...])
@@ -102,12 +128,26 @@
         hidden_proj[c] = total[c * rows : (c + 1) * rows]
 
 
-def logits_kernel(order, twin, *refs):
+def logits_kernel(order, twin, offsets, *refs):
     n = len(order)
-    pieces, unembeds = refs[:n], refs[n : n + twin]
-    target_column, weights, in_part, out, placed, placed_target = refs[n + twin :]
-    rows = pieces[0].shape[0]
-    normed = jnp.concatenate([piece[...] for piece in pieces], axis=0)
+    own, refs = refs[0], refs[1:]
+    rows, width = own.shape
+    blocks = [[own[...]]]
+    if n > 1:
+        count = n - 2
+        early, parts, gain, refs = refs[:count], refs[count : count + n], refs[count + n], refs[count + n + 1 :]
+        own_gain = gain[:, pl.ds(pl.multiple_of(offsets[0](), 128), width)]
+        for raw, part in zip(early, parts[1:-1], strict=True):
+            tail = part[:, -128:].astype(F32)
+            inverse = tail[:, 0:1] + tail[:, 32:33] + tail[:, 64:65]
+            blocks[0].append((raw[...].astype(F32) * own_gain * inverse).astype(BF16))
+        blocks[0].append(parts[-1][:, -width:])
+        for k in range(1, len(offsets)):
+            blocks.append([part[:, (k - 1) * width : k * width] for part in parts])
+    unembeds = refs[:twin]
+    target_column, weights, in_part, out, placed, placed_target = refs[twin:]
+    blocks = [jnp.concatenate(block, axis=0) for block in blocks]
+    slices = [pl.ds(pl.multiple_of(offset(), 128), width) for offset in offsets]
     entries = unembeds[0].shape[0]
     mine, own = lax.axis_index("dp"), lax.axis_size("vocab")
     starts = [(pl.multiple_of(local(), 16), pl.multiple_of(whole(), 16)) for local, whole in order]
@@ -115,7 +155,7 @@
         placed_target[pl.ds(local, rows), :] = target_column[pl.ds(whole, rows), :]
     logits, onehot = [], []
     for u, unembed in enumerate(unembeds):
-        relative = dot(unembed[...], normed, ((1,), (1,))).T
+        relative = sum(dot(unembed[:, at], block, ((1,), (1,))) for at, block in zip(slices, blocks, strict=True)).T
         for k, (local, _) in enumerate(starts):
             placed[u, pl.ds(local, rows), :] = relative[k * rows : (k + 1) * rows]
         logits.append(placed[u])
@@ -227,9 +267,7 @@
 
 
 def swap(x, size, mask):
-    vocab = size["vocab"]
-    count = size["dp"] * vocab
-    return lax.ppermute(x, AXES, [(i, i ^ mask) for i in range(count)])
+    return lax.ppermute(x, AXES, [(i, i ^ mask) for i in range(size["dp"] * size["vocab"])])
 
 
 def body(size, *args):
@@ -252,40 +290,49 @@
     twin = 2 if fast else 1
     row_shape = sds((n_vocab, per_device, projected), F32)
 
-    def norm(row_pieces, offsets):
+    def norm(row_pieces, offsets, rest=()):
         return call(
-            functools.partial(norm_kernel, offsets), (sds((rows, features), BF16), row_shape), len(row_pieces) + 1
+            functools.partial(norm_kernel, offsets),
+            (row_shape, sds((rows, row_pieces[0].shape[1]), BF16), *rest),
+            len(row_pieces) + 1,
         )(*row_pieces, gain_row)
 
-    sources = (hidden, gain_row, proj_out, unembed, proj_in, inputs, targets.reshape(1, tokens))
-    shapes = [sds(x.shape, x.dtype) for x in sources]
-    shapes[4] = sds((inputs.shape[1], projected), BF16)
-    hidden_here, gain_row, proj_out, unembed_here, proj_slice, inputs, target_row = call(
+    hidden_here, gain_row = call(
         stage_kernel,
-        tuple(shapes),
-        len(sources),
-        hbm_at=range(len(sources)),
-        scratch=[pltpu.SemaphoreType.DMA((len(sources),))],
-    )(*sources)
+        (sds(hidden.shape, BF16), sds(gain_row.shape, F32)),
+        2,
+        hbm_at=(0, 1),
+        scratch=[pltpu.SemaphoreType.DMA((2,))],
+    )(hidden, gain_row)
 
     def side_work(row_pieces, offsets, others):
+        n = len(row_pieces) + len(others)
+        sources = (proj_out, unembed, proj_in, inputs, targets.reshape(1, tokens))
+        shapes = [pltpu.VMEM(x.shape, x.dtype) for x in sources]
+        shapes[2] = pltpu.VMEM((inputs.shape[1], projected), BF16)
         return call(
             functools.partial(side_kernel, offsets, len(others)),
             (sds((twin, entries, projected), F32), row_shape, row_shape, sds((tokens, 128), F32)),
-            len(row_pieces) + len(others) + 6,
+            n + 6,
+            hbm_at=range(n, n + 5),
+            scratch=shapes + [pltpu.SemaphoreType.DMA((5,))],
             us=4.0,
-        )(*row_pieces, *others, proj_out, unembed_here, proj_slice, inputs, target_row, gain_row)
+        )(*row_pieces, *others, *sources, gain_row)
 
     if fast:
         row_pieces = [swap(hidden, size, k) for k in (2, 3, 1)]
+        masks = (0, 6, 4, 2)
+        early = [swap(hidden, size, r * n_vocab) for r in masks[1:-1]]
         others = [swap(unembed, size, n_vocab)]
         row_pieces = [hidden_here] + row_pieces
         offsets = [lambda k=k: (lax.axis_index("vocab") ^ k) * width for k in (0, 2, 3, 1)]
-        normed, root_mean = norm(row_pieces, offsets)
-        *row_pieces, _ = lax.optimization_barrier((*row_pieces, normed))
+        shapes = sds((rows, features - width + 128), BF16), sds((rows, features), BF16)
+        root_mean, own, rest, whole = norm(row_pieces, offsets, shapes)
+        *row_pieces, _ = lax.optimization_barrier((*row_pieces, own))
         side = side_work(row_pieces, offsets, others)
-        masks = (0, 6, 4, 2)
-        pieces = [normed] + [swap(normed, size, r * n_vocab) for r in masks[1:]]
+        late = [swap(rest, size, r * n_vocab) for r in masks[1:-1]]
+        late.append(swap(whole, size, masks[-1] * n_vocab))
+        pieces = [own, *early, rest, *late, gain_row]
         order = [
             (
                 lambda r=r: (lax.axis_index("dp") ^ r) // 2 * rows,
@@ -296,18 +343,18 @@
     else:
         row_pieces = [lax.all_gather(hidden, "vocab", axis=1, tiled=True)]
         offsets, others = [lambda: 0], []
-        normed, root_mean = norm(row_pieces, offsets)
+        root_mean, own = norm(row_pieces, offsets)
         side = side_work(row_pieces, offsets, others)
-        pieces = [lax.all_gather(normed, "dp", axis=0, tiled=True)]
+        pieces = [lax.all_gather(own, "dp", axis=0, tiled=True)]
         order = [(lambda: 0, lambda: 0)]
     weights, in_part, hidden_proj, target_column = side
     partial = call(
-        functools.partial(logits_kernel, order, twin),
+        functools.partial(logits_kernel, order, twin, offsets),
         sds((devices, 4 * per_device, projected), BF16),
         len(pieces) + twin + 3,
         scratch=[pltpu.VMEM((twin, tokens // twin, entries), F32), pltpu.VMEM((tokens // twin, 128), F32)],
         us=2.0,
-    )(*pieces, unembed_here, *others, target_column, weights, in_part)
+    )(*pieces, unembed, *others, target_column, weights, in_part)
     partial = lax.all_to_all(partial, AXES, 0, 0, tiled=True)
     partial = partial.reshape(n_dp // twin, twin, n_vocab, 4 * per_device, projected)
     merged, logprob = call(

time: 46.1 us -> 48.5 us (1.052)
  starting transfers between devices: 9.34 us -> 12.3 us
  blocking collectives: 19.5 us -> 22.1 us
  waiting for transfers between devices: 7.52 us -> 5.22 us
  Pallas kernels: 8.93 us -> 7.91 us
    ppermute x7 -> x9, starting transfers between devices: 9.34 us -> 12.3 us  [swap(): lax.ppermute(x, AXES, [(i, i ^ mask) for i in range(size['dp'] * size['vo...]
    all_to_all x1, blocking collectives: 10.3 us -> 12.9 us  [steps(): partial = lax.all_to_all(partial, AXES, 0, 0, tiled=True)]
    ppermute x7 -> x9, waiting for transfers between devices: 7.52 us -> 5.22 us  [swap(): lax.ppermute(x, AXES, [(i, i ^ mask) for i in range(size['dp'] * size['vo...]
    pallas_call x6, Pallas kernels: 8.93 us -> 7.91 us  [placed(): run(*[pltpu.with_memory_space_constraint(x, pltpu.HBM) if i in hbm_at els...]
  transfers between devices with their start and end apart: 7 -> 9, of which waited for: 4 -> 2; matrix products, arithmetic and copies ran while one was open for 0% -> 0% of each run, Pallas kernels for 11% -> 9%
where the time goes in v3:
time: 48.5 us; the launch traced here: 48.2 us
  blocking collectives  22.1 us (46%)
  starting transfers between devices  12.3 us (25%)
  Pallas kernels  7.91 us (16%)
  waiting for transfers between devices  5.22 us (11%)
  between operations  0.72 us (1%)
    all_to_all x1, blocking collectives, steps(): partial = lax.all_to_all(partial, AXES, 0, 0, tiled=True)  12.9 us
    ppermute x9, starting transfers between devices, swap(): lax.ppermute(x, AXES, [(i, i ^ mask) for i in range(size['dp'] * size['vo...  12.3 us
    all_to_all x1, blocking collectives, steps(): merged = lax.all_to_all(merged, AXES, 0, 0, tiled=True)  9.19 us
    pallas_call x6, Pallas kernels, placed(): run(*[pltpu.with_memory_space_constraint(x, pltpu.HBM) if i in hbm_at els...  7.91 us
    ppermute x9, waiting for transfers between devices, swap(): lax.ppermute(x, AXES, [(i, i ^ mask) for i in range(size['dp'] * size['vo...  5.22 us
  transfers between devices with their start and end apart: 9, of which 2 were waited for; matrix products, arithmetic and copies ran while one was open for 0% of the time, Pallas kernels for 9%

profile of v3, /device:TPU:0, one launch (start us, length us, event | category | flops | bytes accessed | tf_op | source)
XLA Modules:
  0.0 48.2 jit_solution(10140661136023119875)
XLA Ops:
  0.6 0.6 %collective-permute-start.8 = (bf16[200,5120]{1,0:T(8,128)(2,1)}, bf16[200,5120]{1,0:T(8,128)(2,1)S(1)}, u32[]{:S(2)}, u32[]{:S(2)}) collective-permute-start(bf16[200,5120]{1,0:T(8,128)(2,1)} %refs_8_.3), channel_id=1, source_target_pairs={{0,4},{1,5},{2,6},{3,7},{4,0},{5,1},{6,2},{7,3},{8,12},{9,13},{10,... | collective-permute-start | bytes 6144008 | tf_op jit(solution)/shard_map/ppermute | solution.py:270
  1.2 3.7 %collective-permute-start = (bf16[16,1280]{1,0:T(8,128)(2,1)}, bf16[16,1280]{1,0:T(8,128)(2,1)S(1)}, u32[]{:S(2)}, u32[]{:S(2)}) collective-permute-start(bf16[16,1280]{1,0:T(8,128)(2,1)} %refs_0_.1), channel_id=1, source_target_pairs={{0,2},{1,3},{2,0},{3,1},{4,6},{5,7},{6,4},{7,5},{8,10},{9,11},{10,... | collective-permute-start | bytes 122888 | tf_op jit(solution)/shard_map/ppermute | solution.py:270
  4.8 1.3 %collective-permute-start.1 = (bf16[16,1280]{1,0:T(8,128)(2,1)}, bf16[16,1280]{1,0:T(8,128)(2,1)S(1)}, u32[]{:S(2)}, u32[]{:S(2)}) collective-permute-start(bf16[16,1280]{1,0:T(8,128)(2,1)} %refs_0_.1), channel_id=1, source_target_pairs={{0,3},{1,2},{2,1},{3,0},{4,7},{5,6},{6,5},{7,4},{8,11},{9,10},{10,... | collective-permute-start | bytes 122888 | tf_op jit(solution)/shard_map/ppermute | solution.py:270
  6.2 0.2 collective-permute-start.2
  6.4 0.8 %shard_map.104 = (bf16[16,1280]{1,0:T(8,128)(2,1)S(1)}, f32[1,5120]{1,0:T(1,128)S(1)}) custom-call(bf16[16,1280]{1,0:T(8,128)(2,1)} %refs_0_.1, f32[1,5120]{1,0:T(1,128)} %bitcast.7), custom_call_target="tpu_custom_call" | custom-call | bytes 3000000 | tf_op jit(solution)/shard_map/pallas_call | solution.py:44
  7.3 0.0 collective-permute-done.refs_1_
  7.3 3.6 %collective-permute-done.1.refs_2_ = bf16[16,1280]{1,0:T(8,128)(2,1)S(1)} collective-permute-done((bf16[16,1280]{1,0:T(8,128)(2,1)}, bf16[16,1280]{1,0:T(8,128)(2,1)S(1)}, u32[]{:S(2)}, u32[]{:S(2)}) %collective-permute-start.1) | collective-permute-done | bytes 40992 | tf_op jit(solution)/shard_map/ppermute | solution.py:270
  10.9 0.0 collective-permute-done.2.refs_3_
  10.9 0.2 shard_map.105
  11.1 1.6 %collective-permute-start.7 = (bf16[16,5120]{1,0:T(8,128)(2,1)S(1)}, bf16[16,5120]{1,0:T(8,128)(2,1)S(1)}, u32[]{:S(2)}, u32[]{:S(2)}) collective-permute-start(bf16[16,5120]{1,0:T(8,128)(2,1)S(1)} %get-tuple-element.24), channel_id=1, source_target_pairs={{0,8},{1,9},{2,10},{3,11},{4,12},{5,13},{6,14},{7,15},{8,0},{9,1},... | collective-permute-start | bytes 491528 | tf_op jit(solution)/shard_map/ppermute | solution.py:270
  12.7 1.5 %collective-permute-start.5 = (bf16[16,3968]{1,0:T(8,128)(2,1)S(1)}, bf16[16,3968]{1,0:T(8,128)(2,1)S(1)}, u32[]{:S(2)}, u32[]{:S(2)}) collective-permute-start(bf16[16,3968]{1,0:T(8,128)(2,1)S(1)} %get-tuple-element.23.refs_3_), channel_id=1, source_target_pairs={{0,24},{1,25},{2,26},{3,27},{4,28},{5,29},{6,30},{7,31},{8,16},{9,... | collective-permute-start | bytes 380936 | tf_op jit(solution)/shard_map/ppermute | solution.py:270
  14.2 0.5 %collective-permute-start.6 = (bf16[16,3968]{1,0:T(8,128)(2,1)S(1)}, bf16[16,3968]{1,0:T(8,128)(2,1)S(1)}, u32[]{:S(2)}, u32[]{:S(2)}) collective-permute-start(bf16[16,3968]{1,0:T(8,128)(2,1)S(1)} %get-tuple-element.23.refs_3_), channel_id=1, source_target_pairs={{0,16},{1,17},{2,18},{3,19},{4,20},{5,21},{6,22},{7,23},{8,24},{9,... | collective-permute-start | bytes 380936 | tf_op jit(solution)/shard_map/ppermute | solution.py:270
  14.7 2.4 %collective-permute-start.3 = (bf16[16,1280]{1,0:T(8,128)(2,1)}, bf16[16,1280]{1,0:T(8,128)(2,1)S(1)}, u32[]{:S(2)}, u32[]{:S(2)}) collective-permute-start(bf16[16,1280]{1,0:T(8,128)(2,1)} %refs_0_.1), channel_id=1, source_target_pairs={{0,24},{1,25},{2,26},{3,27},{4,28},{5,29},{6,30},{7,31},{8,16},{9,... | collective-permute-start | bytes 122888 | tf_op jit(solution)/shard_map/ppermute | solution.py:270
  17.1 0.0 collective-permute-done.8.refs_4_.refs_9_
  17.1 0.5 %collective-permute-start.4 = (bf16[16,1280]{1,0:T(8,128)(2,1)}, bf16[16,1280]{1,0:T(8,128)(2,1)S(1)}, u32[]{:S(2)}, u32[]{:S(2)}) collective-permute-start(bf16[16,1280]{1,0:T(8,128)(2,1)} %refs_0_.1), channel_id=1, source_target_pairs={{0,16},{1,17},{2,18},{3,19},{4,20},{5,21},{6,22},{7,23},{8,24},{9,... | collective-permute-start | bytes 122888 | tf_op jit(solution)/shard_map/ppermute | solution.py:270
  17.6 0.0 copy-start
  17.6 3.3 %shard_map.106 = (f32[2,200,128]{2,1,0:T(8,128)S(1)}, f32[4,4,128]{2,1,0:T(4,128)S(1)}, f32[4,4,128]{2,1,0:T(4,128)S(1)}, f32[128,128]{1,0:T(8,128)S(1)}) custom-call(bf16[16,1280]{1,0:T(8,128)(2,1)S(1)} %get-tuple-element.25.refs_0_, bf16[16,1280]{1,0:T(8,128)(2,1)S(1)} %collective-permute-done.refs_1_, ...), custom_call_target="tpu_custom_call" | custom-call | bytes 12000000 | tf_op jit(solution)/shard_map/pallas_call | solution.py:44
  20.9 0.0 collective-permute-done.3.refs_1_
  20.9 1.5 %collective-permute-done.4.refs_2_ = bf16[16,1280]{1,0:T(8,128)(2,1)S(1)} collective-permute-done((bf16[16,1280]{1,0:T(8,128)(2,1)}, bf16[16,1280]{1,0:T(8,128)(2,1)S(1)}, u32[]{:S(2)}, u32[]{:S(2)}) %collective-permute-start.4) | collective-permute-done | bytes 40992 | tf_op jit(solution)/shard_map/ppermute | solution.py:270
  22.4 0.0 collective-permute-done.5.refs_4_
  22.4 0.0 collective-permute-done.6.refs_5_
  22.5 0.0 collective-permute-done.7.refs_6_
  22.5 0.0 copy-done
  22.5 0.0 copy-start.1
  22.5 0.0 copy-start.2
  22.5 1.8 %shard_map.107 = bf16[32,16,128]{2,1,0:T(8,128)(2,1)S(1)} custom-call(bf16[16,1280]{1,0:T(8,128)(2,1)S(1)} %get-tuple-element.22.refs_0_, bf16[16,1280]{1,0:T(8,128)(2,1)S(1)} %collective-permute-done.3.refs_1_, bf16[16,1280]{1,0:T(8,128)(2,1)S(1)} %collective-permute-done.4.refs_2_, bf16[16,3968]{1,0:T(8,128)(2,1)S(1)} %get-tuple-element.23.refs_3_, ...), custom_call_target="tpu_custom_call" | custom-call | bytes 6000000 | tf_op jit(solution)/shard_map/pallas_call | solution.py:44
  24.3 12.9 %all_to_all.10 = bf16[32,16,128]{2,1,0:T(8,128)(2,1)S(1)} all-to-all(bf16[32,16,128]{2,1,0:T(8,128)(2,1)S(1)} %shard_map.107), channel_id=1, replica_groups=mesh['dp'=8,'vocab'=4] {'dp','vocab'}, dimensions={0} | all-to-all | bytes 262144 | tf_op jit(solution)/shard_map/all_to_all | solution.py:358
  37.2 0.3 shard_map.108
  37.5 9.2 %all_to_all.11.parts = bf16[32,8,128]{2,1,0:T(8,128)(2,1)S(1)} all-to-all(bf16[32,8,128]{2,1,0:T(8,128)(2,1)S(1)} %get-tuple-element.34), channel_id=1, replica_groups=mesh['dp'=8,'vocab'=4] {'dp','vocab'}, dimensions={0} | all-to-all | bytes 131072 | tf_op jit(solution)/shard_map/all_to_all | solution.py:365
  46.7 0.0 copy-done.1
  46.7 0.0 copy-done.2
  46.7 1.5 %shard_map.109 = (f32[4,64]{1,0:T(4,128)}, f32[1,16]{1,0:T(1,128)}) custom-call(bf16[32,8,128]{2,1,0:T(8,128)(2,1)S(1)} %all_to_all.11.parts, s32[1,128]{1,0:T(1,128)S(1)} %bitcast.6, bf16[64,16384]{1,0:T(8,128)(2,1)S(1)} %copy-done.1, f32[1,16]{1,0:T(1,128)S(1)} %get-tuple-element.35.logprob_in), custom_call_target="tpu_custom_call" | custom-call | bytes 3000000 | tf_op jit(solution)/shard_map/pallas_call | solution.py:44
Async XLA Ops:
  0.6 16.5 %collective-permute-start.8 = (bf16[200,5120]{1,0:T(8,128)(2,1)}, bf16[200,5120]{1,0:T(8,128)(2,1)S(1)}, u32[]{:S(2)}, u32[]{:S(2)}) collective-permute-start(bf16[200,5120]{1,0:T(8,128)(2,1)} %refs_8_.3), channel_id=1, source_target_pairs={{0,4},{1,5},{2,6},{3,7},{4,0},{5,1},{6,2},{7,3},{8,12},{9,13},{10,... | collective-permute-start | bytes 6144008 | tf_op jit(solution)/shard_map/ppermute | solution.py:270
  1.2 6.1 %collective-permute-start = (bf16[16,1280]{1,0:T(8,128)(2,1)}, bf16[16,1280]{1,0:T(8,128)(2,1)S(1)}, u32[]{:S(2)}, u32[]{:S(2)}) collective-permute-start(bf16[16,1280]{1,0:T(8,128)(2,1)} %refs_0_.1), channel_id=1, source_target_pairs={{0,2},{1,3},{2,0},{3,1},{4,6},{5,7},{6,4},{7,5},{8,10},{9,11},{10,... | collective-permute-start | bytes 122888 | tf_op jit(solution)/shard_map/ppermute | solution.py:270
  4.8 6.1 %collective-permute-start.1 = (bf16[16,1280]{1,0:T(8,128)(2,1)}, bf16[16,1280]{1,0:T(8,128)(2,1)S(1)}, u32[]{:S(2)}, u32[]{:S(2)}) collective-permute-start(bf16[16,1280]{1,0:T(8,128)(2,1)} %refs_0_.1), channel_id=1, source_target_pairs={{0,3},{1,2},{2,1},{3,0},{4,7},{5,6},{6,5},{7,4},{8,11},{9,10},{10,... | collective-permute-start | bytes 122888 | tf_op jit(solution)/shard_map/ppermute | solution.py:270
  6.2 4.8 %collective-permute-start.2 = (bf16[16,1280]{1,0:T(8,128)(2,1)}, bf16[16,1280]{1,0:T(8,128)(2,1)S(1)}, u32[]{:S(2)}, u32[]{:S(2)}) collective-permute-start(bf16[16,1280]{1,0:T(8,128)(2,1)} %refs_0_.1), channel_id=1, source_target_pairs={{0,1},{1,0},{2,3},{3,2},{4,5},{5,4},{6,7},{7,6},{8,9},{9,8},{10,11... | collective-permute-start | bytes 122888 | tf_op jit(solution)/shard_map/ppermute | solution.py:270
  11.1 11.3 %collective-permute-start.7 = (bf16[16,5120]{1,0:T(8,128)(2,1)S(1)}, bf16[16,5120]{1,0:T(8,128)(2,1)S(1)}, u32[]{:S(2)}, u32[]{:S(2)}) collective-permute-start(bf16[16,5120]{1,0:T(8,128)(2,1)S(1)} %get-tuple-element.24), channel_id=1, source_target_pairs={{0,8},{1,9},{2,10},{3,11},{4,12},{5,13},{6,14},{7,15},{8,0},{9,1},... | collective-permute-start | bytes 491528 | tf_op jit(solution)/shard_map/ppermute | solution.py:270
  12.7 9.8 %collective-permute-start.5 = (bf16[16,3968]{1,0:T(8,128)(2,1)S(1)}, bf16[16,3968]{1,0:T(8,128)(2,1)S(1)}, u32[]{:S(2)}, u32[]{:S(2)}) collective-permute-start(bf16[16,3968]{1,0:T(8,128)(2,1)S(1)} %get-tuple-element.23.refs_3_), channel_id=1, source_target_pairs={{0,24},{1,25},{2,26},{3,27},{4,28},{5,29},{6,30},{7,31},{8,16},{9,... | collective-permute-start | bytes 380936 | tf_op jit(solution)/shard_map/ppermute | solution.py:270
  14.2 8.3 %collective-permute-start.6 = (bf16[16,3968]{1,0:T(8,128)(2,1)S(1)}, bf16[16,3968]{1,0:T(8,128)(2,1)S(1)}, u32[]{:S(2)}, u32[]{:S(2)}) collective-permute-start(bf16[16,3968]{1,0:T(8,128)(2,1)S(1)} %get-tuple-element.23.refs_3_), channel_id=1, source_target_pairs={{0,16},{1,17},{2,18},{3,19},{4,20},{5,21},{6,22},{7,23},{8,24},{9,... | collective-permute-start | bytes 380936 | tf_op jit(solution)/shard_map/ppermute | solution.py:270
  14.7 6.2 %collective-permute-start.3 = (bf16[16,1280]{1,0:T(8,128)(2,1)}, bf16[16,1280]{1,0:T(8,128)(2,1)S(1)}, u32[]{:S(2)}, u32[]{:S(2)}) collective-permute-start(bf16[16,1280]{1,0:T(8,128)(2,1)} %refs_0_.1), channel_id=1, source_target_pairs={{0,24},{1,25},{2,26},{3,27},{4,28},{5,29},{6,30},{7,31},{8,16},{9,... | collective-permute-start | bytes 122888 | tf_op jit(solution)/shard_map/ppermute | solution.py:270
  17.1 5.3 %collective-permute-start.4 = (bf16[16,1280]{1,0:T(8,128)(2,1)}, bf16[16,1280]{1,0:T(8,128)(2,1)S(1)}, u32[]{:S(2)}, u32[]{:S(2)}) collective-permute-start(bf16[16,1280]{1,0:T(8,128)(2,1)} %refs_0_.1), channel_id=1, source_target_pairs={{0,16},{1,17},{2,18},{3,19},{4,20},{5,21},{6,22},{7,23},{8,24},{9,... | collective-permute-start | bytes 122888 | tf_op jit(solution)/shard_map/ppermute | solution.py:270
  17.6 4.8 %copy-start = (bf16[200,5120]{1,0:T(8,128)(2,1)S(1)}, bf16[200,5120]{1,0:T(8,128)(2,1)}, u32[]{:S(2)}) copy-start(bf16[200,5120]{1,0:T(8,128)(2,1)} %refs_8_.3) | copy-start | bytes 6144004
  22.5 24.2 %copy-start.1 = (bf16[64,16384]{1,0:T(8,128)(2,1)S(1)}, bf16[64,16384]{1,0:T(8,128)(2,1)}, u32[]{:S(2)}) copy-start(bf16[64,16384]{1,0:T(8,128)(2,1)} %store.1) | copy-start | bytes 6291460
  22.5 24.2 %copy-start.2 = (s32[128]{0:T(128)S(1)}, s32[128]{0:T(128)}, u32[]{:S(2)}) copy-start(s32[128]{0:T(128)} %param.16) | copy-start | bytes 1540

commit v4 on v3

--- a/solution.py
+++ b/solution.py
@@ -145,23 +145,20 @@
         for k in range(1, len(offsets)):
             blocks.append([part[:, (k - 1) * width : k * width] for part in parts])
     unembeds = refs[:twin]
-    target_column, weights, in_part, out, placed, placed_target = refs[twin:]
+    target_column, weights, in_part, out = refs[twin:]
     blocks = [jnp.concatenate(block, axis=0) for block in blocks]
     slices = [pl.ds(pl.multiple_of(offset(), 128), width) for offset in offsets]
     entries = unembeds[0].shape[0]
-    mine, own = lax.axis_index("dp"), lax.axis_size("vocab")
-    starts = [(pl.multiple_of(local(), 16), pl.multiple_of(whole(), 16)) for local, whole in order]
-    for local, whole in starts:
-        placed_target[pl.ds(local, rows), :] = target_column[pl.ds(whole, rows), :]
+    mine, own_count = lax.axis_index("dp"), lax.axis_size("vocab")
+    target = [target_column[pl.ds(pl.multiple_of(whole(), 16), rows), 0:1] for _, whole in order]
+    target = jnp.concatenate(target, axis=0)
     logits, onehot = [], []
     for u, unembed in enumerate(unembeds):
         relative = sum(dot(unembed[:, at], block, ((1,), (1,))) for at, block in zip(slices, blocks, strict=True)).T
-        for k, (local, _) in enumerate(starts):
-            placed[u, pl.ds(local, rows), :] = relative[k * rows : (k + 1) * rows]
-        logits.append(placed[u])
-        place = (mine ^ u) * own + lax.axis_index("vocab")
+        logits.append(relative)
+        place = (mine ^ u) * own_count + lax.axis_index("vocab")
         column = lax.broadcasted_iota(jnp.int32, relative.shape, 1) + place * entries
-        onehot.append(placed_target[:, 0:1] == column.astype(F32))
+        onehot.append(target == column.astype(F32))
     tokens = logits[0].shape[0]
     peak = functools.reduce(jnp.maximum, [jnp.max(x, axis=1, keepdims=True) for x in logits])
     total = moment = target_logit = sums = target_row = 0.0
@@ -171,11 +168,12 @@
         total = total + jnp.sum(other, axis=1, keepdims=True)
         moment = moment + jnp.sum(other * shifted, axis=1, keepdims=True)
         target_logit = target_logit + jnp.sum(jnp.where(onehot[u], logits[u], 0.0), axis=1, keepdims=True)
-        w_high, w_low = split(weights[u])
+        w_high = weights[u].astype(BF16)
         p_high, p_low = split(other)
-        sums = sums + (dot(p_high, w_high) + (dot(p_high, w_low) + dot(p_low, w_high)))
         hot = onehot[u].astype(F32).astype(BF16)
-        target_row = target_row + dot(hot, w_high)
+        stacked = dot(jnp.concatenate([p_high, hot, p_low], axis=0), w_high)
+        sums = sums + (stacked[:tokens] + stacked[2 * tokens :])
+        target_row = target_row + stacked[tokens : 2 * tokens]
     lane = lax.broadcasted_iota(jnp.int32, (tokens, 128), 1)
     which = (lane // 2) % 4
     stats = jnp.where(which < 2, jnp.where(which == 0, peak, total), jnp.where(which == 2, moment, target_logit))
@@ -184,19 +182,21 @@
     low = stats - high - middle
     piece = (lane // 8) % 4
     stats = jnp.where(piece == 0, high, jnp.where(piece == 1, middle, jnp.where(piece == 2, low, 0.0)))
-    chunks = out.shape[0]
-    rows = tokens * twin // chunks
-    block = lax.broadcasted_iota(jnp.int32, (rows, 128), 1) // (128 // own)
-    for d in range(chunks // own):
-        first = d // twin * own
-        row_stats = stats[first * rows : (first + 1) * rows]
-        for k in range(1, own):
-            row_stats = jnp.where(block == k, stats[(first + k) * rows : (first + k + 1) * rows], row_stats)
-        for k in range(own):
-            here = slice((first + k) * rows, (first + k + 1) * rows)
-            terms = jnp.where(mine == d, in_part[k], 0.0)
-            packed = jnp.concatenate([sums[here], target_row[here], terms, row_stats], axis=0)
-            out[d * own + k] = packed.astype(BF16)
+    tile = in_part.shape[1]
+    block = lax.broadcasted_iota(jnp.int32, (tile, 128), 1) // (128 // own_count)
+    for k, (local, _) in enumerate(order):
+        for g in range(rows // (own_count * tile)):
+            base = k * rows + g * own_count * tile
+            row_stats = stats[base : base + tile]
+            for c in range(1, own_count):
+                row_stats = jnp.where(block == c, stats[base + c * tile : base + (c + 1) * tile], row_stats)
+            for e in range(twin):
+                row = (local() // (own_count * tile) + g) * twin + e
+                for c in range(own_count):
+                    here = slice(base + c * tile, base + (c + 1) * tile)
+                    terms = jnp.where(mine == row, in_part[c], 0.0)
+                    packed = jnp.concatenate([sums[here], target_row[here], terms, row_stats], axis=0)
+                    out[row * own_count + c] = packed.astype(BF16)
 
 
 def merge_kernel(features, parts, hidden_projs, root_means, out, logprob):
@@ -352,7 +352,6 @@
         functools.partial(logits_kernel, order, twin, offsets),
         sds((devices, 4 * per_device, projected), BF16),
         len(pieces) + twin + 3,
-        scratch=[pltpu.VMEM((twin, tokens // twin, entries), F32), pltpu.VMEM((tokens // twin, 128), F32)],
         us=2.0,
     )(*pieces, unembed, *others, target_column, weights, in_part)
     partial = lax.all_to_all(partial, AXES, 0, 0, tiled=True)

time: 48.5 us -> 48.2 us (level)
  no operation moved by 1% of the time
where the time goes in v4:
time: 48.2 us; the launch traced here: 48 us
  blocking collectives  22.1 us (46%)
  starting transfers between devices  12.3 us (26%)
  Pallas kernels  7.7 us (16%)
  waiting for transfers between devices  5.22 us (11%)
  between operations  0.72 us (1%)
    all_to_all x1, blocking collectives, steps(): partial = lax.all_to_all(partial, AXES, 0, 0, tiled=True)  12.9 us
    ppermute x9, starting transfers between devices, swap(): lax.ppermute(x, AXES, [(i, i ^ mask) for i in range(size['dp'] * size['vo...  12.3 us
    all_to_all x1, blocking collectives, steps(): merged = lax.all_to_all(merged, AXES, 0, 0, tiled=True)  9.19 us
    pallas_call x6, Pallas kernels, placed(): run(*[pltpu.with_memory_space_constraint(x, pltpu.HBM) if i in hbm_at els...  7.7 us
    ppermute x9, waiting for transfers between devices, swap(): lax.ppermute(x, AXES, [(i, i ^ mask) for i in range(size['dp'] * size['vo...  5.22 us
  transfers between devices with their start and end apart: 9, of which 2 were waited for; matrix products, arithmetic and copies ran while one was open for 0% of the time, Pallas kernels for 9%

profile of v4, /device:TPU:0, one launch (start us, length us, event | category | flops | bytes accessed | tf_op | source)
XLA Modules:
  0.0 48.0 jit_solution(13719014960247269525)
XLA Ops:
  0.6 0.6 %collective-permute-start.8 = (bf16[200,5120]{1,0:T(8,128)(2,1)}, bf16[200,5120]{1,0:T(8,128)(2,1)S(1)}, u32[]{:S(2)}, u32[]{:S(2)}) collective-permute-start(bf16[200,5120]{1,0:T(8,128)(2,1)} %refs_8_.3), channel_id=1, source_target_pairs={{0,4},{1,5},{2,6},{3,7},{4,0},{5,1},{6,2},{7,3},{8,12},{9,13},{10,... | collective-permute-start | bytes 6144008 | tf_op jit(solution)/shard_map/ppermute | solution.py:270
  1.2 3.7 %collective-permute-start = (bf16[16,1280]{1,0:T(8,128)(2,1)}, bf16[16,1280]{1,0:T(8,128)(2,1)S(1)}, u32[]{:S(2)}, u32[]{:S(2)}) collective-permute-start(bf16[16,1280]{1,0:T(8,128)(2,1)} %refs_0_.1), channel_id=1, source_target_pairs={{0,2},{1,3},{2,0},{3,1},{4,6},{5,7},{6,4},{7,5},{8,10},{9,11},{10,... | collective-permute-start | bytes 122888 | tf_op jit(solution)/shard_map/ppermute | solution.py:270
  4.8 1.3 %collective-permute-start.1 = (bf16[16,1280]{1,0:T(8,128)(2,1)}, bf16[16,1280]{1,0:T(8,128)(2,1)S(1)}, u32[]{:S(2)}, u32[]{:S(2)}) collective-permute-start(bf16[16,1280]{1,0:T(8,128)(2,1)} %refs_0_.1), channel_id=1, source_target_pairs={{0,3},{1,2},{2,1},{3,0},{4,7},{5,6},{6,5},{7,4},{8,11},{9,10},{10,... | collective-permute-start | bytes 122888 | tf_op jit(solution)/shard_map/ppermute | solution.py:270
  6.2 0.2 collective-permute-start.2
  6.4 0.8 %shard_map.104 = (bf16[16,1280]{1,0:T(8,128)(2,1)S(1)}, f32[1,5120]{1,0:T(1,128)S(1)}) custom-call(bf16[16,1280]{1,0:T(8,128)(2,1)} %refs_0_.1, f32[1,5120]{1,0:T(1,128)} %bitcast.7), custom_call_target="tpu_custom_call" | custom-call | bytes 3000000 | tf_op jit(solution)/shard_map/pallas_call | solution.py:44
  7.3 0.0 collective-permute-done.refs_1_
  7.3 3.6 %collective-permute-done.1.refs_2_ = bf16[16,1280]{1,0:T(8,128)(2,1)S(1)} collective-permute-done((bf16[16,1280]{1,0:T(8,128)(2,1)}, bf16[16,1280]{1,0:T(8,128)(2,1)S(1)}, u32[]{:S(2)}, u32[]{:S(2)}) %collective-permute-start.1) | collective-permute-done | bytes 40992 | tf_op jit(solution)/shard_map/ppermute | solution.py:270
  10.9 0.0 collective-permute-done.2.refs_3_
  10.9 0.2 shard_map.105
  11.1 1.6 %collective-permute-start.7 = (bf16[16,5120]{1,0:T(8,128)(2,1)S(1)}, bf16[16,5120]{1,0:T(8,128)(2,1)S(1)}, u32[]{:S(2)}, u32[]{:S(2)}) collective-permute-start(bf16[16,5120]{1,0:T(8,128)(2,1)S(1)} %get-tuple-element.24), channel_id=1, source_target_pairs={{0,8},{1,9},{2,10},{3,11},{4,12},{5,13},{6,14},{7,15},{8,0},{9,1},... | collective-permute-start | bytes 491528 | tf_op jit(solution)/shard_map/ppermute | solution.py:270
  12.7 1.5 %collective-permute-start.5 = (bf16[16,3968]{1,0:T(8,128)(2,1)S(1)}, bf16[16,3968]{1,0:T(8,128)(2,1)S(1)}, u32[]{:S(2)}, u32[]{:S(2)}) collective-permute-start(bf16[16,3968]{1,0:T(8,128)(2,1)S(1)} %get-tuple-element.23.refs_3_), channel_id=1, source_target_pairs={{0,24},{1,25},{2,26},{3,27},{4,28},{5,29},{6,30},{7,31},{8,16},{9,... | collective-permute-start | bytes 380936 | tf_op jit(solution)/shard_map/ppermute | solution.py:270
  14.2 0.5 %collective-permute-start.6 = (bf16[16,3968]{1,0:T(8,128)(2,1)S(1)}, bf16[16,3968]{1,0:T(8,128)(2,1)S(1)}, u32[]{:S(2)}, u32[]{:S(2)}) collective-permute-start(bf16[16,3968]{1,0:T(8,128)(2,1)S(1)} %get-tuple-element.23.refs_3_), channel_id=1, source_target_pairs={{0,16},{1,17},{2,18},{3,19},{4,20},{5,21},{6,22},{7,23},{8,24},{9,... | collective-permute-start | bytes 380936 | tf_op jit(solution)/shard_map/ppermute | solution.py:270
  14.7 2.4 %collective-permute-start.3 = (bf16[16,1280]{1,0:T(8,128)(2,1)}, bf16[16,1280]{1,0:T(8,128)(2,1)S(1)}, u32[]{:S(2)}, u32[]{:S(2)}) collective-permute-start(bf16[16,1280]{1,0:T(8,128)(2,1)} %refs_0_.1), channel_id=1, source_target_pairs={{0,24},{1,25},{2,26},{3,27},{4,28},{5,29},{6,30},{7,31},{8,16},{9,... | collective-permute-start | bytes 122888 | tf_op jit(solution)/shard_map/ppermute | solution.py:270
  17.1 0.0 collective-permute-done.8.refs_4_.refs_9_
  17.1 0.5 %collective-permute-start.4 = (bf16[16,1280]{1,0:T(8,128)(2,1)}, bf16[16,1280]{1,0:T(8,128)(2,1)S(1)}, u32[]{:S(2)}, u32[]{:S(2)}) collective-permute-start(bf16[16,1280]{1,0:T(8,128)(2,1)} %refs_0_.1), channel_id=1, source_target_pairs={{0,16},{1,17},{2,18},{3,19},{4,20},{5,21},{6,22},{7,23},{8,24},{9,... | collective-permute-start | bytes 122888 | tf_op jit(solution)/shard_map/ppermute | solution.py:270
  17.6 0.0 copy-start
  17.6 3.3 %shard_map.106 = (f32[2,200,128]{2,1,0:T(8,128)S(1)}, f32[4,4,128]{2,1,0:T(4,128)S(1)}, f32[4,4,128]{2,1,0:T(4,128)S(1)}, f32[128,128]{1,0:T(8,128)S(1)}) custom-call(bf16[16,1280]{1,0:T(8,128)(2,1)S(1)} %get-tuple-element.25.refs_0_, bf16[16,1280]{1,0:T(8,128)(2,1)S(1)} %collective-permute-done.refs_1_, ...), custom_call_target="tpu_custom_call" | custom-call | bytes 12000000 | tf_op jit(solution)/shard_map/pallas_call | solution.py:44
  20.9 0.0 collective-permute-done.3.refs_1_
  20.9 1.5 %collective-permute-done.4.refs_2_ = bf16[16,1280]{1,0:T(8,128)(2,1)S(1)} collective-permute-done((bf16[16,1280]{1,0:T(8,128)(2,1)}, bf16[16,1280]{1,0:T(8,128)(2,1)S(1)}, u32[]{:S(2)}, u32[]{:S(2)}) %collective-permute-start.4) | collective-permute-done | bytes 40992 | tf_op jit(solution)/shard_map/ppermute | solution.py:270
  22.4 0.0 collective-permute-done.5.refs_4_
  22.4 0.0 collective-permute-done.6.refs_5_
  22.5 0.0 collective-permute-done.7.refs_6_
  22.5 0.0 copy-done
  22.5 0.0 copy-start.1
  22.5 0.0 copy-start.2
  22.5 1.6 %shard_map.107 = bf16[32,16,128]{2,1,0:T(8,128)(2,1)S(1)} custom-call(bf16[16,1280]{1,0:T(8,128)(2,1)S(1)} %get-tuple-element.22.refs_0_, bf16[16,1280]{1,0:T(8,128)(2,1)S(1)} %collective-permute-done.3.refs_1_, bf16[16,1280]{1,0:T(8,128)(2,1)S(1)} %collective-permute-done.4.refs_2_, bf16[16,3968]{1,0:T(8,128)(2,1)S(1)} %get-tuple-element.23.refs_3_, ...), custom_call_target="tpu_custom_call" | custom-call | bytes 6000000 | tf_op jit(solution)/shard_map/pallas_call | solution.py:44
  24.1 12.9 %all_to_all.10 = bf16[32,16,128]{2,1,0:T(8,128)(2,1)S(1)} all-to-all(bf16[32,16,128]{2,1,0:T(8,128)(2,1)S(1)} %shard_map.107), channel_id=1, replica_groups=mesh['dp'=8,'vocab'=4] {'dp','vocab'}, dimensions={0} | all-to-all | bytes 262144 | tf_op jit(solution)/shard_map/all_to_all | solution.py:357
  37.0 0.3 shard_map.108
  37.3 9.2 %all_to_all.11.parts = bf16[32,8,128]{2,1,0:T(8,128)(2,1)S(1)} all-to-all(bf16[32,8,128]{2,1,0:T(8,128)(2,1)S(1)} %get-tuple-element.34), channel_id=1, replica_groups=mesh['dp'=8,'vocab'=4] {'dp','vocab'}, dimensions={0} | all-to-all | bytes 131072 | tf_op jit(solution)/shard_map/all_to_all | solution.py:364
  46.5 0.0 copy-done.1
  46.5 0.0 copy-done.2
  46.5 1.5 %shard_map.109 = (f32[4,64]{1,0:T(4,128)}, f32[1,16]{1,0:T(1,128)}) custom-call(bf16[32,8,128]{2,1,0:T(8,128)(2,1)S(1)} %all_to_all.11.parts, s32[1,128]{1,0:T(1,128)S(1)} %bitcast.6, bf16[64,16384]{1,0:T(8,128)(2,1)S(1)} %copy-done.1, f32[1,16]{1,0:T(1,128)S(1)} %get-tuple-element.35.logprob_in), custom_call_target="tpu_custom_call" | custom-call | bytes 3000000 | tf_op jit(solution)/shard_map/pallas_call | solution.py:44
Async XLA Ops:
  0.6 16.5 %collective-permute-start.8 = (bf16[200,5120]{1,0:T(8,128)(2,1)}, bf16[200,5120]{1,0:T(8,128)(2,1)S(1)}, u32[]{:S(2)}, u32[]{:S(2)}) collective-permute-start(bf16[200,5120]{1,0:T(8,128)(2,1)} %refs_8_.3), channel_id=1, source_target_pairs={{0,4},{1,5},{2,6},{3,7},{4,0},{5,1},{6,2},{7,3},{8,12},{9,13},{10,... | collective-permute-start | bytes 6144008 | tf_op jit(solution)/shard_map/ppermute | solution.py:270
  1.2 6.1 %collective-permute-start = (bf16[16,1280]{1,0:T(8,128)(2,1)}, bf16[16,1280]{1,0:T(8,128)(2,1)S(1)}, u32[]{:S(2)}, u32[]{:S(2)}) collective-permute-start(bf16[16,1280]{1,0:T(8,128)(2,1)} %refs_0_.1), channel_id=1, source_target_pairs={{0,2},{1,3},{2,0},{3,1},{4,6},{5,7},{6,4},{7,5},{8,10},{9,11},{10,... | collective-permute-start | bytes 122888 | tf_op jit(solution)/shard_map/ppermute | solution.py:270
  4.8 6.1 %collective-permute-start.1 = (bf16[16,1280]{1,0:T(8,128)(2,1)}, bf16[16,1280]{1,0:T(8,128)(2,1)S(1)}, u32[]{:S(2)}, u32[]{:S(2)}) collective-permute-start(bf16[16,1280]{1,0:T(8,128)(2,1)} %refs_0_.1), channel_id=1, source_target_pairs={{0,3},{1,2},{2,1},{3,0},{4,7},{5,6},{6,5},{7,4},{8,11},{9,10},{10,... | collective-permute-start | bytes 122888 | tf_op jit(solution)/shard_map/ppermute | solution.py:270
  6.2 4.8 %collective-permute-start.2 = (bf16[16,1280]{1,0:T(8,128)(2,1)}, bf16[16,1280]{1,0:T(8,128)(2,1)S(1)}, u32[]{:S(2)}, u32[]{:S(2)}) collective-permute-start(bf16[16,1280]{1,0:T(8,128)(2,1)} %refs_0_.1), channel_id=1, source_target_pairs={{0,1},{1,0},{2,3},{3,2},{4,5},{5,4},{6,7},{7,6},{8,9},{9,8},{10,11... | collective-permute-start | bytes 122888 | tf_op jit(solution)/shard_map/ppermute | solution.py:270
  11.1 11.3 %collective-permute-start.7 = (bf16[16,5120]{1,0:T(8,128)(2,1)S(1)}, bf16[16,5120]{1,0:T(8,128)(2,1)S(1)}, u32[]{:S(2)}, u32[]{:S(2)}) collective-permute-start(bf16[16,5120]{1,0:T(8,128)(2,1)S(1)} %get-tuple-element.24), channel_id=1, source_target_pairs={{0,8},{1,9},{2,10},{3,11},{4,12},{5,13},{6,14},{7,15},{8,0},{9,1},... | collective-permute-start | bytes 491528 | tf_op jit(solution)/shard_map/ppermute | solution.py:270
  12.7 9.8 %collective-permute-start.5 = (bf16[16,3968]{1,0:T(8,128)(2,1)S(1)}, bf16[16,3968]{1,0:T(8,128)(2,1)S(1)}, u32[]{:S(2)}, u32[]{:S(2)}) collective-permute-start(bf16[16,3968]{1,0:T(8,128)(2,1)S(1)} %get-tuple-element.23.refs_3_), channel_id=1, source_target_pairs={{0,24},{1,25},{2,26},{3,27},{4,28},{5,29},{6,30},{7,31},{8,16},{9,... | collective-permute-start | bytes 380936 | tf_op jit(solution)/shard_map/ppermute | solution.py:270
  14.2 8.3 %collective-permute-start.6 = (bf16[16,3968]{1,0:T(8,128)(2,1)S(1)}, bf16[16,3968]{1,0:T(8,128)(2,1)S(1)}, u32[]{:S(2)}, u32[]{:S(2)}) collective-permute-start(bf16[16,3968]{1,0:T(8,128)(2,1)S(1)} %get-tuple-element.23.refs_3_), channel_id=1, source_target_pairs={{0,16},{1,17},{2,18},{3,19},{4,20},{5,21},{6,22},{7,23},{8,24},{9,... | collective-permute-start | bytes 380936 | tf_op jit(solution)/shard_map/ppermute | solution.py:270
  14.7 6.2 %collective-permute-start.3 = (bf16[16,1280]{1,0:T(8,128)(2,1)}, bf16[16,1280]{1,0:T(8,128)(2,1)S(1)}, u32[]{:S(2)}, u32[]{:S(2)}) collective-permute-start(bf16[16,1280]{1,0:T(8,128)(2,1)} %refs_0_.1), channel_id=1, source_target_pairs={{0,24},{1,25},{2,26},{3,27},{4,28},{5,29},{6,30},{7,31},{8,16},{9,... | collective-permute-start | bytes 122888 | tf_op jit(solution)/shard_map/ppermute | solution.py:270
  17.1 5.3 %collective-permute-start.4 = (bf16[16,1280]{1,0:T(8,128)(2,1)}, bf16[16,1280]{1,0:T(8,128)(2,1)S(1)}, u32[]{:S(2)}, u32[]{:S(2)}) collective-permute-start(bf16[16,1280]{1,0:T(8,128)(2,1)} %refs_0_.1), channel_id=1, source_target_pairs={{0,16},{1,17},{2,18},{3,19},{4,20},{5,21},{6,22},{7,23},{8,24},{9,... | collective-permute-start | bytes 122888 | tf_op jit(solution)/shard_map/ppermute | solution.py:270
  17.6 4.8 %copy-start = (bf16[200,5120]{1,0:T(8,128)(2,1)S(1)}, bf16[200,5120]{1,0:T(8,128)(2,1)}, u32[]{:S(2)}) copy-start(bf16[200,5120]{1,0:T(8,128)(2,1)} %refs_8_.3) | copy-start | bytes 6144004
  22.5 24.0 %copy-start.1 = (bf16[64,16384]{1,0:T(8,128)(2,1)S(1)}, bf16[64,16384]{1,0:T(8,128)(2,1)}, u32[]{:S(2)}) copy-start(bf16[64,16384]{1,0:T(8,128)(2,1)} %store.1) | copy-start | bytes 6291460
  22.5 24.0 %copy-start.2 = (s32[128]{0:T(128)S(1)}, s32[128]{0:T(128)}, u32[]{:S(2)}) copy-start(s32[128]{0:T(128)} %param.16) | copy-start | bytes 1540

commit v5 on v4

--- a/solution.py
+++ b/solution.py
@@ -97,9 +97,9 @@
 def side_kernel(offsets, others, *refs):
     n = len(offsets)
     pieces, other_unembeds, refs = refs[:n], refs[n : n + others], refs[n + others :]
-    sources, gain = refs[:5], refs[5]
+    sources, inputs, gain = refs[:4], refs[4], refs[5]
     weights, in_part, hidden_proj, target_column = refs[6:10]
-    buffers, sems = refs[10:15], refs[15]
+    buffers, sems = refs[10:14], refs[14]
     copies = []
     for i, (source, buffer) in enumerate(zip(sources, buffers, strict=True)):
         if source.shape != buffer.shape:
@@ -107,7 +107,7 @@
             source = source.at[pl.ds(pl.multiple_of(lax.axis_index("vocab") * width, 16), width), :]
         copies.append(pltpu.make_async_copy(source, buffer, sems.at[i]))
         copies[-1].start()
-    proj_out, unembed, proj_slice, inputs, targets = buffers
+    proj_out, unembed, proj_slice, targets = buffers
     copies[0].wait()
     total = 0.0
     for piece, offset in zip(pieces, offsets, strict=True):
@@ -152,13 +152,20 @@
     mine, own_count = lax.axis_index("dp"), lax.axis_size("vocab")
     target = [target_column[pl.ds(pl.multiple_of(whole(), 16), rows), 0:1] for _, whole in order]
     target = jnp.concatenate(target, axis=0)
-    logits, onehot = [], []
+    sent = target
+    if twin > 1:
+        sent = [
+            target_column[pl.ds(pl.multiple_of((2 * g + 1 - mine % 2) * rows, 16), rows), 0:1] for g in range(n)
+        ]
+        sent = jnp.concatenate(sent, axis=0)
+    logits, onehot, hots = [], [], []
     for u, unembed in enumerate(unembeds):
         relative = sum(dot(unembed[:, at], block, ((1,), (1,))) for at, block in zip(slices, blocks, strict=True)).T
         logits.append(relative)
         place = (mine ^ u) * own_count + lax.axis_index("vocab")
         column = lax.broadcasted_iota(jnp.int32, relative.shape, 1) + place * entries
         onehot.append(target == column.astype(F32))
+        hots.append((sent == column.astype(F32)).astype(F32).astype(BF16))
     tokens = logits[0].shape[0]
     peak = functools.reduce(jnp.maximum, [jnp.max(x, axis=1, keepdims=True) for x in logits])
     total = moment = target_logit = sums = target_row = 0.0
@@ -170,8 +177,7 @@
         target_logit = target_logit + jnp.sum(jnp.where(onehot[u], logits[u], 0.0), axis=1, keepdims=True)
         w_high = weights[u].astype(BF16)
         p_high, p_low = split(other)
-        hot = onehot[u].astype(F32).astype(BF16)
-        stacked = dot(jnp.concatenate([p_high, hot, p_low], axis=0), w_high)
+        stacked = dot(jnp.concatenate([p_high, hots[u], p_low], axis=0), w_high)
         sums = sums + (stacked[:tokens] + stacked[2 * tokens :])
         target_row = target_row + stacked[tokens : 2 * tokens]
     lane = lax.broadcasted_iota(jnp.int32, (tokens, 128), 1)
@@ -190,12 +196,19 @@
             row_stats = stats[base : base + tile]
             for c in range(1, own_count):
                 row_stats = jnp.where(block == c, stats[base + c * tile : base + (c + 1) * tile], row_stats)
-            for e in range(twin):
-                row = (local() // (own_count * tile) + g) * twin + e
-                for c in range(own_count):
-                    here = slice(base + c * tile, base + (c + 1) * tile)
+            row = (local() // (own_count * tile) + g) * twin + mine % twin
+            row_sent = k * twin + 1 - mine % twin
+            for c in range(own_count):
+                here = slice(base + c * tile, base + (c + 1) * tile)
+                packed = [sums[here], row_stats]
+                if twin > 1:
+                    out[row * own_count + c] = jnp.concatenate(packed, axis=0).astype(BF16)
+                    terms = jnp.where(mine ^ 1 == row_sent, in_part[c], 0.0)
+                    packed = jnp.concatenate([target_row[here], terms], axis=0)
+                    out[row_sent * own_count + c] = packed.astype(BF16)
+                else:
                     terms = jnp.where(mine == row, in_part[c], 0.0)
-                    packed = jnp.concatenate([sums[here], target_row[here], terms, row_stats], axis=0)
+                    packed = jnp.concatenate([*packed, target_row[here], terms], axis=0)
                     out[row * own_count + c] = packed.astype(BF16)
 
 
@@ -205,9 +218,16 @@
     root_mean = root_means[index]
     rows = hidden_proj.shape[0]
     chunks = parts.shape[0] * own
-    received = parts[:, lax.axis_index("dp") % parts.shape[1]]
-    received = received.reshape(chunks, *received.shape[2:]).astype(F32)
-    stats = received[:, 3 * rows : 4 * rows].reshape(chunks * rows, 128)
+    twin = parts.shape[1]
+    core = lax.axis_index("dp") % twin
+
+    def take(at):
+        x = parts[:, at]
+        return x.reshape(chunks, *x.shape[2:]).astype(F32)
+
+    received = take(core)
+    sent = take(1 - core) if twin > 1 else received[:, 2 * rows : 4 * rows]
+    stats = received[:, rows : 2 * rows].reshape(chunks * rows, 128)
     stats = stats + pltpu.roll(stats, 128 - 8, 1) + pltpu.roll(stats, 128 - 16, 1)
     shape = (chunks, rows, 128)
     peak, total = stats.reshape(shape), pltpu.roll(stats, 128 - 2, 1).reshape(shape)
@@ -233,13 +253,13 @@
         return jnp.sum(jnp.where(at, x, 0.0), axis=-1, keepdims=True)
 
     weight, rest, slope = pick(weight), pick(rest), pick(slope)
-    target_row = jnp.sum(received[:, rows : 2 * rows], axis=0)
+    target_row = jnp.sum(sent[:, 0:rows], axis=0)
     grad_proj = rest * target_row - jnp.sum(weight * received[:, 0:rows], axis=0)
     grad_dot = root_mean * slope
     out_grad = grad_proj / root_mean - hidden_proj * (
         grad_dot / (features * (root_mean * root_mean * root_mean))
     )
-    in_proj = jnp.sum(received[:, 2 * rows : 3 * rows], axis=0)
+    in_proj = jnp.sum(sent[:, rows : 2 * rows], axis=0)
     both = jnp.concatenate([out_grad, in_proj], axis=0).astype(BF16)
     out[...] = jnp.broadcast_to(both[None], out.shape)
 
@@ -305,31 +325,32 @@
         scratch=[pltpu.SemaphoreType.DMA((2,))],
     )(hidden, gain_row)
 
-    def side_work(row_pieces, offsets, others):
+    def side_work(row_pieces, offsets, others, inputs):
         n = len(row_pieces) + len(others)
-        sources = (proj_out, unembed, proj_in, inputs, targets.reshape(1, tokens))
+        sources = (proj_out, unembed, proj_in, targets.reshape(1, tokens))
         shapes = [pltpu.VMEM(x.shape, x.dtype) for x in sources]
         shapes[2] = pltpu.VMEM((inputs.shape[1], projected), BF16)
         return call(
             functools.partial(side_kernel, offsets, len(others)),
             (sds((twin, entries, projected), F32), row_shape, row_shape, sds((tokens, 128), F32)),
             n + 6,
-            hbm_at=range(n, n + 5),
-            scratch=shapes + [pltpu.SemaphoreType.DMA((5,))],
+            hbm_at=range(n, n + 4),
+            scratch=shapes + [pltpu.SemaphoreType.DMA((4,))],
             us=4.0,
-        )(*row_pieces, *others, *sources, gain_row)
+        )(*row_pieces, *others, *sources, inputs, gain_row)
 
     if fast:
         row_pieces = [swap(hidden, size, k) for k in (2, 3, 1)]
         masks = (0, 6, 4, 2)
         early = [swap(hidden, size, r * n_vocab) for r in masks[1:-1]]
         others = [swap(unembed, size, n_vocab)]
+        inputs = swap(inputs, size, n_vocab)
         row_pieces = [hidden_here] + row_pieces
         offsets = [lambda k=k: (lax.axis_index("vocab") ^ k) * width for k in (0, 2, 3, 1)]
         shapes = sds((rows, features - width + 128), BF16), sds((rows, features), BF16)
         root_mean, own, rest, whole = norm(row_pieces, offsets, shapes)
         *row_pieces, _ = lax.optimization_barrier((*row_pieces, own))
-        side = side_work(row_pieces, offsets, others)
+        side = side_work(row_pieces, offsets, others, inputs)
         late = [swap(rest, size, r * n_vocab) for r in masks[1:-1]]
         late.append(swap(whole, size, masks[-1] * n_vocab))
         pieces = [own, *early, rest, *late, gain_row]
@@ -344,18 +365,18 @@
         row_pieces = [lax.all_gather(hidden, "vocab", axis=1, tiled=True)]
         offsets, others = [lambda: 0], []
         root_mean, own = norm(row_pieces, offsets)
-        side = side_work(row_pieces, offsets, others)
+        side = side_work(row_pieces, offsets, others, inputs)
         pieces = [lax.all_gather(own, "dp", axis=0, tiled=True)]
         order = [(lambda: 0, lambda: 0)]
     weights, in_part, hidden_proj, target_column = side
     partial = call(
         functools.partial(logits_kernel, order, twin, offsets),
-        sds((devices, 4 * per_device, projected), BF16),
+        sds((devices, 4 // twin * per_device, projected), BF16),
         len(pieces) + twin + 3,
         us=2.0,
     )(*pieces, unembed, *others, target_column, weights, in_part)
     partial = lax.all_to_all(partial, AXES, 0, 0, tiled=True)
-    partial = partial.reshape(n_dp // twin, twin, n_vocab, 4 * per_device, projected)
+    partial = partial.reshape(n_dp // twin, twin, n_vocab, 4 // twin * per_device, projected)
     merged, logprob = call(
         functools.partial(merge_kernel, features),
         (sds((devices, 2 * per_device, projected), BF16), sds((1, rows), F32)),

time: 48.2 us -> 47.4 us (0.983)
  blocking collectives: 22.1 us -> 20.9 us
    all_to_all x1, blocking collectives: 12.9 us -> 11.7 us  [steps(): partial = lax.all_to_all(partial, AXES, 0, 0, tiled=True)]
    ppermute x9 -> x10, waiting for transfers between devices: 5.22 us -> 5.52 us  [swap(): lax.ppermute(x, AXES, [(i, i ^ mask) for i in range(size['dp'] * size['vo...]
    ppermute x9 -> x10, starting transfers between devices: 12.3 us -> 12.3 us  [swap(): lax.ppermute(x, AXES, [(i, i ^ mask) for i in range(size['dp'] * size['vo...]
  transfers between devices with their start and end apart: 9 -> 10, of which waited for: 2 -> 3; matrix products, arithmetic and copies ran while one was open for 0% -> 0% of each run, Pallas kernels for 9% -> 9%
where the time goes in v5:
time: 47.4 us; the launch traced here: 47.1 us
  blocking collectives  20.9 us (44%)
  starting transfers between devices  12.3 us (26%)
  Pallas kernels  7.68 us (16%)
  waiting for transfers between devices  5.52 us (12%)
  between operations  0.72 us (2%)
    ppermute x10, starting transfers between devices, swap(): lax.ppermute(x, AXES, [(i, i ^ mask) for i in range(size['dp'] * size['vo...  12.3 us
    all_to_all x1, blocking collectives, steps(): partial = lax.all_to_all(partial, AXES, 0, 0, tiled=True)  11.7 us
    all_to_all x1, blocking collectives, steps(): merged = lax.all_to_all(merged, AXES, 0, 0, tiled=True)  9.19 us
    pallas_call x6, Pallas kernels, placed(): run(*[pltpu.with_memory_space_constraint(x, pltpu.HBM) if i in hbm_at els...  7.68 us
    ppermute x10, waiting for transfers between devices, swap(): lax.ppermute(x, AXES, [(i, i ^ mask) for i in range(size['dp'] * size['vo...  5.52 us
  transfers between devices with their start and end apart: 10, of which 3 were waited for; matrix products, arithmetic and copies ran while one was open for 0% of the time, Pallas kernels for 9%

profile of v5, /device:TPU:0, one launch (start us, length us, event | category | flops | bytes accessed | tf_op | source)
XLA Modules:
  0.0 47.1 jit_solution(10722617165440496809)
XLA Ops:
  0.6 0.6 %collective-permute-start.8 = (bf16[200,5120]{1,0:T(8,128)(2,1)}, bf16[200,5120]{1,0:T(8,128)(2,1)S(1)}, u32[]{:S(2)}, u32[]{:S(2)}) collective-permute-start(bf16[200,5120]{1,0:T(8,128)(2,1)} %refs_8_.1), channel_id=1, source_target_pairs={{0,4},{1,5},{2,6},{3,7},{4,0},{5,1},{6,2},{7,3},{8,12},{9,13},{10,... | collective-permute-start | bytes 6144008 | tf_op jit(solution)/shard_map/ppermute | solution.py:290
  1.2 3.7 %collective-permute-start = (bf16[16,1280]{1,0:T(8,128)(2,1)}, bf16[16,1280]{1,0:T(8,128)(2,1)S(1)}, u32[]{:S(2)}, u32[]{:S(2)}) collective-permute-start(bf16[16,1280]{1,0:T(8,128)(2,1)} %refs_0_.1), channel_id=1, source_target_pairs={{0,2},{1,3},{2,0},{3,1},{4,6},{5,7},{6,4},{7,5},{8,10},{9,11},{10,... | collective-permute-start | bytes 122888 | tf_op jit(solution)/shard_map/ppermute | solution.py:290
  4.8 1.3 %collective-permute-start.1 = (bf16[16,1280]{1,0:T(8,128)(2,1)}, bf16[16,1280]{1,0:T(8,128)(2,1)S(1)}, u32[]{:S(2)}, u32[]{:S(2)}) collective-permute-start(bf16[16,1280]{1,0:T(8,128)(2,1)} %refs_0_.1), channel_id=1, source_target_pairs={{0,3},{1,2},{2,1},{3,0},{4,7},{5,6},{6,5},{7,4},{8,11},{9,10},{10,... | collective-permute-start | bytes 122888 | tf_op jit(solution)/shard_map/ppermute | solution.py:290
  6.2 0.2 collective-permute-start.2
  6.4 0.8 %shard_map.104 = (bf16[16,1280]{1,0:T(8,128)(2,1)S(1)}, f32[1,5120]{1,0:T(1,128)S(1)}) custom-call(bf16[16,1280]{1,0:T(8,128)(2,1)} %refs_0_.1, f32[1,5120]{1,0:T(1,128)} %bitcast.7), custom_call_target="tpu_custom_call" | custom-call | bytes 3000000 | tf_op jit(solution)/shard_map/pallas_call | solution.py:44
  7.3 0.0 collective-permute-done.refs_1_
  7.3 3.6 %collective-permute-done.1.refs_2_ = bf16[16,1280]{1,0:T(8,128)(2,1)S(1)} collective-permute-done((bf16[16,1280]{1,0:T(8,128)(2,1)}, bf16[16,1280]{1,0:T(8,128)(2,1)S(1)}, u32[]{:S(2)}, u32[]{:S(2)}) %collective-permute-start.1) | collective-permute-done | bytes 40992 | tf_op jit(solution)/shard_map/ppermute | solution.py:290
  10.9 0.0 collective-permute-done.2.refs_3_
  10.9 0.2 shard_map.105
  11.1 1.6 %collective-permute-start.7 = (bf16[16,5120]{1,0:T(8,128)(2,1)S(1)}, bf16[16,5120]{1,0:T(8,128)(2,1)S(1)}, u32[]{:S(2)}, u32[]{:S(2)}) collective-permute-start(bf16[16,5120]{1,0:T(8,128)(2,1)S(1)} %get-tuple-element.24), channel_id=1, source_target_pairs={{0,8},{1,9},{2,10},{3,11},{4,12},{5,13},{6,14},{7,15},{8,0},{9,1},... | collective-permute-start | bytes 491528 | tf_op jit(solution)/shard_map/ppermute | solution.py:290
  12.7 1.5 %collective-permute-start.5 = (bf16[16,3968]{1,0:T(8,128)(2,1)S(1)}, bf16[16,3968]{1,0:T(8,128)(2,1)S(1)}, u32[]{:S(2)}, u32[]{:S(2)}) collective-permute-start(bf16[16,3968]{1,0:T(8,128)(2,1)S(1)} %get-tuple-element.23.refs_3_), channel_id=1, source_target_pairs={{0,24},{1,25},{2,26},{3,27},{4,28},{5,29},{6,30},{7,31},{8,16},{9,... | collective-permute-start | bytes 380936 | tf_op jit(solution)/shard_map/ppermute | solution.py:290
  14.2 0.5 %collective-permute-start.6 = (bf16[16,3968]{1,0:T(8,128)(2,1)S(1)}, bf16[16,3968]{1,0:T(8,128)(2,1)S(1)}, u32[]{:S(2)}, u32[]{:S(2)}) collective-permute-start(bf16[16,3968]{1,0:T(8,128)(2,1)S(1)} %get-tuple-element.23.refs_3_), channel_id=1, source_target_pairs={{0,16},{1,17},{2,18},{3,19},{4,20},{5,21},{6,22},{7,23},{8,24},{9,... | collective-permute-start | bytes 380936 | tf_op jit(solution)/shard_map/ppermute | solution.py:290
  14.7 0.0 collective-permute-start.9
  14.7 1.4 %collective-permute-done.9.refs_9_ = bf16[16,768]{1,0:T(8,128)(2,1)S(1)} collective-permute-done((bf16[16,768]{1,0:T(8,128)(2,1)}, bf16[16,768]{1,0:T(8,128)(2,1)S(1)}, u32[]{:S(2)}, u32[]{:S(2)}) %collective-permute-start.9) | collective-permute-done | bytes 24608 | tf_op jit(solution)/shard_map/ppermute | solution.py:290
  16.1 2.4 %collective-permute-start.3 = (bf16[16,1280]{1,0:T(8,128)(2,1)}, bf16[16,1280]{1,0:T(8,128)(2,1)S(1)}, u32[]{:S(2)}, u32[]{:S(2)}) collective-permute-start(bf16[16,1280]{1,0:T(8,128)(2,1)} %refs_0_.1), channel_id=1, source_target_pairs={{0,24},{1,25},{2,26},{3,27},{4,28},{5,29},{6,30},{7,31},{8,16},{9,... | collective-permute-start | bytes 122888 | tf_op jit(solution)/shard_map/ppermute | solution.py:290
  18.5 0.0 collective-permute-done.8.refs_4_.refs_9_
  18.5 0.5 %collective-permute-start.4 = (bf16[16,1280]{1,0:T(8,128)(2,1)}, bf16[16,1280]{1,0:T(8,128)(2,1)S(1)}, u32[]{:S(2)}, u32[]{:S(2)}) collective-permute-start(bf16[16,1280]{1,0:T(8,128)(2,1)} %refs_0_.1), channel_id=1, source_target_pairs={{0,16},{1,17},{2,18},{3,19},{4,20},{5,21},{6,22},{7,23},{8,24},{9,... | collective-permute-start | bytes 122888 | tf_op jit(solution)/shard_map/ppermute | solution.py:290
  19.0 0.0 copy-start
  19.0 3.3 %shard_map.106 = (f32[2,200,128]{2,1,0:T(8,128)S(1)}, f32[4,4,128]{2,1,0:T(4,128)S(1)}, f32[4,4,128]{2,1,0:T(4,128)S(1)}, f32[128,128]{1,0:T(8,128)S(1)}) custom-call(bf16[16,1280]{1,0:T(8,128)(2,1)S(1)} %get-tuple-element.25.refs_0_, bf16[16,1280]{1,0:T(8,128)(2,1)S(1)} %collective-permute-done.refs_1_, ...), custom_call_target="tpu_custom_call" | custom-call | bytes 12000000 | tf_op jit(solution)/shard_map/pallas_call | solution.py:44
  22.3 0.0 collective-permute-done.3.refs_1_
  22.3 0.4 collective-permute-done.4.refs_2_
  22.7 0.0 collective-permute-done.5.refs_4_
  22.7 0.0 collective-permute-done.6.refs_5_
  22.7 0.0 collective-permute-done.7.refs_6_
  22.8 0.0 copy-done
  22.8 0.0 copy-start.1
  22.8 0.0 copy-start.2
  22.8 1.6 %shard_map.107 = bf16[32,8,128]{2,1,0:T(8,128)(2,1)S(1)} custom-call(bf16[16,1280]{1,0:T(8,128)(2,1)S(1)} %get-tuple-element.22.refs_0_, bf16[16,1280]{1,0:T(8,128)(2,1)S(1)} %collective-permute-done.3.refs_1_, bf16[16,1280]{1,0:T(8,128)(2,1)S(1)} %collective-permute-done.4.refs_2_, bf16[16,3968]{1,0:T(8,128)(2,1)S(1)} %get-tuple-element.23.refs_3_, ...), custom_call_target="tpu_custom_call" | custom-call | bytes 6000000 | tf_op jit(solution)/shard_map/pallas_call | solution.py:44
  24.4 11.7 %all_to_all.10 = bf16[32,8,128]{2,1,0:T(8,128)(2,1)S(1)} all-to-all(bf16[32,8,128]{2,1,0:T(8,128)(2,1)S(1)} %shard_map.107), channel_id=1, replica_groups=mesh['dp'=8,'vocab'=4] {'dp','vocab'}, dimensions={0} | all-to-all | bytes 131072 | tf_op jit(solution)/shard_map/all_to_all | solution.py:378
  36.1 0.3 shard_map.108
  36.4 9.2 %all_to_all.11.parts = bf16[32,8,128]{2,1,0:T(8,128)(2,1)S(1)} all-to-all(bf16[32,8,128]{2,1,0:T(8,128)(2,1)S(1)} %get-tuple-element.34), channel_id=1, replica_groups=mesh['dp'=8,'vocab'=4] {'dp','vocab'}, dimensions={0} | all-to-all | bytes 131072 | tf_op jit(solution)/shard_map/all_to_all | solution.py:385
  45.6 0.0 copy-done.1
  45.6 0.0 copy-done.2
  45.6 1.5 %shard_map.109 = (f32[4,64]{1,0:T(4,128)}, f32[1,16]{1,0:T(1,128)}) custom-call(bf16[32,8,128]{2,1,0:T(8,128)(2,1)S(1)} %all_to_all.11.parts, s32[1,128]{1,0:T(1,128)S(1)} %bitcast.6, bf16[64,16384]{1,0:T(8,128)(2,1)S(1)} %copy-done.1, f32[1,16]{1,0:T(1,128)S(1)} %get-tuple-element.35.logprob_in), custom_call_target="tpu_custom_call" | custom-call | bytes 3000000 | tf_op jit(solution)/shard_map/pallas_call | solution.py:44
Async XLA Ops:
  0.6 17.9 %collective-permute-start.8 = (bf16[200,5120]{1,0:T(8,128)(2,1)}, bf16[200,5120]{1,0:T(8,128)(2,1)S(1)}, u32[]{:S(2)}, u32[]{:S(2)}) collective-permute-start(bf16[200,5120]{1,0:T(8,128)(2,1)} %refs_8_.1), channel_id=1, source_target_pairs={{0,4},{1,5},{2,6},{3,7},{4,0},{5,1},{6,2},{7,3},{8,12},{9,13},{10,... | collective-permute-start | bytes 6144008 | tf_op jit(solution)/shard_map/ppermute | solution.py:290
  1.2 6.1 %collective-permute-start = (bf16[16,1280]{1,0:T(8,128)(2,1)}, bf16[16,1280]{1,0:T(8,128)(2,1)S(1)}, u32[]{:S(2)}, u32[]{:S(2)}) collective-permute-start(bf16[16,1280]{1,0:T(8,128)(2,1)} %refs_0_.1), channel_id=1, source_target_pairs={{0,2},{1,3},{2,0},{3,1},{4,6},{5,7},{6,4},{7,5},{8,10},{9,11},{10,... | collective-permute-start | bytes 122888 | tf_op jit(solution)/shard_map/ppermute | solution.py:290
  4.8 6.1 %collective-permute-start.1 = (bf16[16,1280]{1,0:T(8,128)(2,1)}, bf16[16,1280]{1,0:T(8,128)(2,1)S(1)}, u32[]{:S(2)}, u32[]{:S(2)}) collective-permute-start(bf16[16,1280]{1,0:T(8,128)(2,1)} %refs_0_.1), channel_id=1, source_target_pairs={{0,3},{1,2},{2,1},{3,0},{4,7},{5,6},{6,5},{7,4},{8,11},{9,10},{10,... | collective-permute-start | bytes 122888 | tf_op jit(solution)/shard_map/ppermute | solution.py:290
  6.2 4.8 %collective-permute-start.2 = (bf16[16,1280]{1,0:T(8,128)(2,1)}, bf16[16,1280]{1,0:T(8,128)(2,1)S(1)}, u32[]{:S(2)}, u32[]{:S(2)}) collective-permute-start(bf16[16,1280]{1,0:T(8,128)(2,1)} %refs_0_.1), channel_id=1, source_target_pairs={{0,1},{1,0},{2,3},{3,2},{4,5},{5,4},{6,7},{7,6},{8,9},{9,8},{10,11... | collective-permute-start | bytes 122888 | tf_op jit(solution)/shard_map/ppermute | solution.py:290
  11.1 11.6 %collective-permute-start.7 = (bf16[16,5120]{1,0:T(8,128)(2,1)S(1)}, bf16[16,5120]{1,0:T(8,128)(2,1)S(1)}, u32[]{:S(2)}, u32[]{:S(2)}) collective-permute-start(bf16[16,5120]{1,0:T(8,128)(2,1)S(1)} %get-tuple-element.24), channel_id=1, source_target_pairs={{0,8},{1,9},{2,10},{3,11},{4,12},{5,13},{6,14},{7,15},{8,0},{9,1},... | collective-permute-start | bytes 491528 | tf_op jit(solution)/shard_map/ppermute | solution.py:290
  12.7 10.1 %collective-permute-start.5 = (bf16[16,3968]{1,0:T(8,128)(2,1)S(1)}, bf16[16,3968]{1,0:T(8,128)(2,1)S(1)}, u32[]{:S(2)}, u32[]{:S(2)}) collective-permute-start(bf16[16,3968]{1,0:T(8,128)(2,1)S(1)} %get-tuple-element.23.refs_3_), channel_id=1, source_target_pairs={{0,24},{1,25},{2,26},{3,27},{4,28},{5,29},{6,30},{7,31},{8,16},{9,... | collective-permute-start | bytes 380936 | tf_op jit(solution)/shard_map/ppermute | solution.py:290
  14.2 8.6 %collective-permute-start.6 = (bf16[16,3968]{1,0:T(8,128)(2,1)S(1)}, bf16[16,3968]{1,0:T(8,128)(2,1)S(1)}, u32[]{:S(2)}, u32[]{:S(2)}) collective-permute-start(bf16[16,3968]{1,0:T(8,128)(2,1)S(1)} %get-tuple-element.23.refs_3_), channel_id=1, source_target_pairs={{0,16},{1,17},{2,18},{3,19},{4,20},{5,21},{6,22},{7,23},{8,24},{9,... | collective-permute-start | bytes 380936 | tf_op jit(solution)/shard_map/ppermute | solution.py:290
  14.7 1.4 %collective-permute-start.9 = (bf16[16,768]{1,0:T(8,128)(2,1)}, bf16[16,768]{1,0:T(8,128)(2,1)S(1)}, u32[]{:S(2)}, u32[]{:S(2)}) collective-permute-start(bf16[16,768]{1,0:T(8,128)(2,1)} %param.10), channel_id=1, source_target_pairs={{0,4},{1,5},{2,6},{3,7},{4,0},{5,1},{6,2},{7,3},{8,12},{9,13},{10,... | collective-permute-start | bytes 73736 | tf_op jit(solution)/shard_map/ppermute | solution.py:290
  16.1 6.2 %collective-permute-start.3 = (bf16[16,1280]{1,0:T(8,128)(2,1)}, bf16[16,1280]{1,0:T(8,128)(2,1)S(1)}, u32[]{:S(2)}, u32[]{:S(2)}) collective-permute-start(bf16[16,1280]{1,0:T(8,128)(2,1)} %refs_0_.1), channel_id=1, source_target_pairs={{0,24},{1,25},{2,26},{3,27},{4,28},{5,29},{6,30},{7,31},{8,16},{9,... | collective-permute-start | bytes 122888 | tf_op jit(solution)/shard_map/ppermute | solution.py:290
  18.5 4.2 %collective-permute-start.4 = (bf16[16,1280]{1,0:T(8,128)(2,1)}, bf16[16,1280]{1,0:T(8,128)(2,1)S(1)}, u32[]{:S(2)}, u32[]{:S(2)}) collective-permute-start(bf16[16,1280]{1,0:T(8,128)(2,1)} %refs_0_.1), channel_id=1, source_target_pairs={{0,16},{1,17},{2,18},{3,19},{4,20},{5,21},{6,22},{7,23},{8,24},{9,... | collective-permute-start | bytes 122888 | tf_op jit(solution)/shard_map/ppermute | solution.py:290
  19.0 3.7 %copy-start = (bf16[200,5120]{1,0:T(8,128)(2,1)S(1)}, bf16[200,5120]{1,0:T(8,128)(2,1)}, u32[]{:S(2)}) copy-start(bf16[200,5120]{1,0:T(8,128)(2,1)} %refs_8_.1) | copy-start | bytes 6144004
  22.8 22.8 %copy-start.1 = (bf16[64,16384]{1,0:T(8,128)(2,1)S(1)}, bf16[64,16384]{1,0:T(8,128)(2,1)}, u32[]{:S(2)}) copy-start(bf16[64,16384]{1,0:T(8,128)(2,1)} %store.1) | copy-start | bytes 6291460
  22.8 22.8 %copy-start.2 = (s32[128]{0:T(128)S(1)}, s32[128]{0:T(128)}, u32[]{:S(2)}) copy-start(s32[128]{0:T(128)} %param.16) | copy-start | bytes 1540
